TPU v7x, 512 devices: a whole 4x8x8 slice. The times are simulated.
512 devices in a mesh: gx: 32 (over x, z), gy: 8 (over y_lo, core), phys: 2 (over y_hi).
Axes of the slice: x: 4, y: 8 (y_hi: 2, y_lo: 4; y = y_hi * 4 + y_lo), z: 8, core: 2. Of those that a mesh axis runs over, the one named last changes fastest.
Arguments:
- mech_load: float32 [32, 8, 2, 128, 768], P('gx', 'gy', 'phys'), may hold values from -63 to 63
- heat_load: float32 [32, 8, 2, 128, 256], P('gx', 'gy', 'phys'), may hold values from -63 to 63
- mech_factor: bfloat16 [32, 8, 2, 768, 768], P('gx', 'gy', 'phys'), may hold values from -0.21875 to 0.21875
- heat_factor: bfloat16 [32, 8, 2, 256, 256], P('gx', 'gy', 'phys'), may hold values from -0.375 to 0.375
- mech_diag: float32 [32, 8, 2, 768], P('gx', 'gy', 'phys'), may hold values from 0.1 to 1
- heat_diag: float32 [32, 8, 2, 256], P('gx', 'gy', 'phys'), may hold values from 0.1 to 1
- mech_wx: float32 [32, 8, 2, 768], P('gx', 'gy', 'phys'), may hold values from 0.5 to 4
- mech_wy: float32 [32, 8, 2, 768], P('gx', 'gy', 'phys'), may hold values from 0.5 to 4
- mech_wp: float32 [32, 8, 768], P('gx', 'gy'), may hold values from 0.5 to 4
- heat_wx: float32 [32, 8, 2, 256], P('gx', 'gy', 'phys'), may hold values from 0.5 to 4
- heat_wy: float32 [32, 8, 2, 256], P('gx', 'gy', 'phys'), may hold values from 0.5 to 4
- heat_wp: float32 [32, 8, 256], P('gx', 'gy'), may hold values from 0.5 to 4
- coupling: bfloat16 [32, 8, 2, 768, 256], P('gx', 'gy', 'phys'), may hold values from -0.21875 to 0.21875
- mech_sens: bfloat16 [32, 8, 2, 768, 256], P('gx', 'gy', 'phys'), may hold values from -0.21875 to 0.21875
- heat_sens: bfloat16 [32, 8, 2, 256, 256], P('gx', 'gy', 'phys'), may hold values from -0.375 to 0.375
- density: float32 [32, 8, 256], P('gx', 'gy', 'phys'), may hold values from 0.2 to 1
- material_ids: int32 [32, 8, 256], P('gx', 'gy', 'phys'), may hold values from 0 to 7
- material_scale: float32 [8], replicated, may hold values from 1 to 10
Outputs:
- mech_adjoint: float32 [32, 8, 2, 128, 768], P('gx', 'gy', 'phys')
- heat_adjoint: float32 [32, 8, 2, 128, 256], P('gx', 'gy', 'phys')
- gradient: float32 [32, 8, 256], P('gx', 'gy', 'phys')
All inputs are finite; a program needn't handle non-finite values.
Results may differ from a plain program's by a relative error of at most 0.014.
Values may be sent and summed in bfloat16 or wider, within the bound.
A program may use at most 64 MiB of HBM per device.

v0:
```python
import jax
import jax.numpy as jnp
from jax import lax
from jax.sharding import PartitionSpec as P

LOADS = 128
ITERS = 2


def with_halo(array, sides, width):
    for axis, dim in sides:
        devices, length = (lax.axis_size(axis), array.shape[dim])
        up = [(i, (i + 1) % devices) for i in range(devices - 1)]
        down = [(j, i) for i, j in up]
        last = lax.slice_in_dim(array, length - width, length, axis=dim)
        initial = lax.slice_in_dim(array, 0, width, axis=dim)
        before = lax.ppermute(last, axis, up)
        after = lax.ppermute(initial, axis, down)
        array = jnp.concatenate([before, array, after], axis=dim)
    return array


def from_partner(array, axis, apart):
    return lax.ppermute(array, axis, [(i, i ^ 1 << apart) for i in range(lax.axis_size(axis))])


def from_behind(array, axis, by):
    devices = lax.axis_size(axis)
    pairs = [(i, i + by) for i in range(devices) if 0 <= i + by < devices]
    return lax.ppermute(array, axis, pairs)


def apply_operator(rounded, coefs, thermal):
    factor, diagonal, lower_x, upper_x, lower_y, upper_y, partner_weight = coefs
    block = rounded[None, None, None]
    if thermal:
        padded = with_halo(block, (("gx", 0), ("gy", 1)), 1)
        partner = from_partner(rounded, "phys", 0)
    else:
        padded = with_halo(block, (("gx", 0), ("gy", 1)), 1)
        partner = from_partner(rounded, "phys", 0)
    middle = 0
    western = padded[0, 1, middle].astype(jnp.float32)
    eastern = padded[2, 1, middle].astype(jnp.float32)
    southern = padded[1, 0, middle].astype(jnp.float32)
    northern = padded[1, 2, middle].astype(jnp.float32)
    inner = jnp.dot(rounded, factor, preferred_element_type=jnp.float32).astype(jnp.bfloat16)
    schur = lax.dot_general(
        inner, factor, (((1,), (1,)), ((), ())), preferred_element_type=jnp.float32
    )
    values = rounded.astype(jnp.float32)
    image = schur + diagonal * values
    image = image + lower_x * (values - western) + upper_x * (values - eastern)
    image = image + lower_y * (values - southern) + upper_y * (values - northern)
    image = image + partner_weight * (values - partner.astype(jnp.float32))
    return image


def interface_solve(load, coefs, thermal):
    solution = jnp.zeros_like(load)
    residual = load
    direction = load
    if thermal:
        current = lax.psum(jnp.sum(load * load, axis=1), ("gx", "gy", "phys"))
    else:
        current = lax.psum(jnp.sum(load * load, axis=1), ("gx", "gy", "phys"))
    for iteration in range(ITERS):
        rounded = direction.astype(jnp.bfloat16)
        image = apply_operator(rounded, coefs, thermal)
        local_curv = jnp.sum(rounded.astype(jnp.float32) * image, axis=1)
        if thermal:
            curvature = lax.psum(local_curv, ("gx", "gy", "phys"))
        else:
            curvature = lax.psum(local_curv, ("gx", "gy", "phys"))
        alpha = current / curvature
        solution = solution + alpha[:, None] * direction
        if iteration + 1 < ITERS:
            residual = residual - alpha[:, None] * image
            if thermal:
                following = lax.psum(jnp.sum(residual * residual, axis=1), ("gx", "gy", "phys"))
            else:
                following = lax.psum(jnp.sum(residual * residual, axis=1), ("gx", "gy", "phys"))
            direction = residual + (following / current)[:, None] * direction
            current = following
    return solution


def on_device(
    mech_load,
    heat_load,
    mech_factor,
    heat_factor,
    mech_diag,
    heat_diag,
    mech_wx,
    mech_wy,
    mech_wp,
    heat_wx,
    heat_wy,
    heat_wp,
    coupling,
    mech_sens,
    heat_sens,
    density,
    material_ids,
    material_scale,
):
    mech_width = mech_load.shape[-1]
    lower_rows = jnp.concatenate([mech_wx[0, 0, 0], heat_wx[0, 0, 0]])
    lower_cols = jnp.concatenate([mech_wy[0, 0, 0], heat_wy[0, 0, 0]])
    upper_rows = from_behind(lower_rows, "gx", -1)
    upper_cols = from_behind(lower_cols, "gy", -1)
    mech_coefs = (
        mech_factor[0, 0, 0],
        mech_diag[0, 0, 0],
        mech_wx[0, 0, 0],
        upper_rows[:mech_width],
        mech_wy[0, 0, 0],
        upper_cols[:mech_width],
        mech_wp[0, 0],
    )
    mech_adjoint = interface_solve(mech_load[0, 0, 0], mech_coefs, False)
    coupled = jnp.dot(
        mech_adjoint.astype(jnp.bfloat16), coupling[0, 0, 0], preferred_element_type=jnp.float32
    )
    heat_source = heat_load[0, 0, 0] - coupled
    heat_coefs = (
        heat_factor[0, 0, 0],
        heat_diag[0, 0, 0],
        heat_wx[0, 0, 0],
        upper_rows[mech_width:],
        heat_wy[0, 0, 0],
        upper_cols[mech_width:],
        heat_wp[0, 0],
    )
    heat_adjoint = interface_solve(heat_source, heat_coefs, True)
    mech_energy = jnp.sum(mech_adjoint * mech_adjoint, axis=0).astype(jnp.bfloat16)
    heat_energy = jnp.sum(heat_adjoint * heat_adjoint, axis=0).astype(jnp.bfloat16)
    partial_sens = jnp.dot(mech_energy, mech_sens[0, 0, 0], preferred_element_type=jnp.float32)
    partial_sens = partial_sens + jnp.dot(
        heat_energy, heat_sens[0, 0, 0], preferred_element_type=jnp.float32
    )
    summed = lax.psum(partial_sens, "phys")
    stride = partial_sens.shape[0] // lax.axis_size("phys")
    portion = lax.dynamic_slice_in_dim(summed, lax.axis_index("phys") * stride, stride, 0)
    onehot = (
        material_ids[0, 0][:, None] == jnp.arange(material_scale.shape[0], dtype=jnp.int32)[None, :]
    ).astype(jnp.float32)
    stiffness = jnp.dot(onehot, material_scale, precision=lax.Precision.HIGHEST)
    densities = density[0, 0]
    gradient = -3.0 * densities * densities * stiffness * portion / LOADS
    return (mech_adjoint[None, None, None], heat_adjoint[None, None, None], gradient[None, None])


def solution(mesh):
    placed = (
        P("gx", "gy", "phys", None, None),
        P("gx", "gy", "phys", None, None),
        P("gx", "gy", "phys", None, None),
        P("gx", "gy", "phys", None, None),
        P("gx", "gy", "phys", None),
        P("gx", "gy", "phys", None),
        P("gx", "gy", "phys", None),
        P("gx", "gy", "phys", None),
        P("gx", "gy", None),
        P("gx", "gy", "phys", None),
        P("gx", "gy", "phys", None),
        P("gx", "gy", None),
        P("gx", "gy", "phys", None, None),
        P("gx", "gy", "phys", None, None),
        P("gx", "gy", "phys", None, None),
        P("gx", "gy", "phys"),
        P("gx", "gy", "phys"),
        P(),
    )
    return jax.shard_map(
        on_device,
        mesh=mesh,
        in_specs=placed,
        out_specs=(
            P("gx", "gy", "phys", None, None),
            P("gx", "gy", "phys", None, None),
            P("gx", "gy", "phys"),
        ),
        check_vma=False,
    )
```

profile of v0, /device:TPU:1, one launch (start us, length us, event | category | flops | bytes accessed | tf_op | source)
XLA Modules:
  0.0 722.6 jit_solution(3888469934136934606)
XLA Ops:
  2.0 4.8 collective-permute-start
  9.4 4.5 collective-permute-done.2
  13.9 5.9 collective-permute-start.3
  23.8 6.5 collective-permute-start.6
  31.9 3.9 collective-permute-done.1
  38.1 107.8 %all-reduce.1 = (f32[128]{0:T(128)S(1)}, f32[128]{0:T(128)S(1)}) all-reduce(f32[128]{0:T(128)S(1)} %fusion.44, f32[128]{0:T(128)S(1)} %get-tuple-element.15), channel_id=1, replica_groups=mesh['gx'=32,'gy'=8,'phys'=2] {'gx','gy','phys'}, use_global_device_ids=true, to_apply=%region_1.0 | all-reduce | flops 256 | bytes 2048 | tf_op jit(solution)/shard_map/psum | solution.py:66
  146.1 94.5 %psum.65 = f32[128]{0:T(128)S(1)} all-reduce(f32[128]{0:T(128)S(1)} %multiply_reduce_fusion.1), channel_id=1, replica_groups=mesh['gx'=32,'gy'=8,'phys'=2] {'gx','gy','phys'}, use_global_device_ids=true, to_apply=%region_5.0 | all-reduce | flops 128 | bytes 1024 | tf_op jit(solution)/shard_map/psum | solution.py:82
  247.1 3.8 collective-permute-done.8
  250.9 3.8 collective-permute-start.10
  256.7 4.7 collective-permute-start.11
  262.1 11.8 %collective-permute-done.11 = bf16[128,768]{1,0:T(8,128)(2,1)} collective-permute-done((bf16[128,768]{1,0:T(8,128)(2,1)S(1)}, bf16[128,768]{1,0:T(8,128)(2,1)}, u32[]{:S(2)}, u32[]{:S(2)}) %collective-permute-start.11) | collective-permute-done | bytes 196640 | tf_op jit(solution)/shard_map/ppermute | solution.py:24
  275.6 98.5 %psum.66 = f32[128]{0:T(128)S(1)} all-reduce(f32[128]{0:T(128)S(1)} %fusion.47), channel_id=1, replica_groups=mesh['gx'=32,'gy'=8,'phys'=2] {'gx','gy','phys'}, use_global_device_ids=true, to_apply=%region_7.0 | all-reduce | flops 128 | bytes 1024 | tf_op jit(solution)/shard_map/psum | solution.py:74
  374.7 3.4 collective-permute-start.12
  379.4 3.7 collective-permute-done.13
  383.1 2.9 collective-permute-start.14
  388.5 4.4 collective-permute-start.16
  394.3 3.8 collective-permute-done.16
  399.6 99.2 %all-reduce = (f32[128]{0:T(128)S(1)}, f32[128]{0:T(128)S(1)}) all-reduce(f32[128]{0:T(128)S(1)} %get-tuple-element.13, f32[128]{0:T(128)S(1)} %get-tuple-element.18), channel_id=1, replica_groups=mesh['gx'=32,'gy'=8,'phys'=2] {'gx','gy','phys'}, use_global_device_ids=true, to_apply=%region_9.0 | all-reduce | flops 256 | bytes 2048 | tf_op jit(solution)/shard_map/psum | solution.py:64
  499.0 95.5 %psum.69 = f32[128]{0:T(128)S(1)} all-reduce(f32[128]{0:T(128)S(1)} %multiply_reduce_fusion.3), channel_id=1, replica_groups=mesh['gx'=32,'gy'=8,'phys'=2] {'gx','gy','phys'}, use_global_device_ids=true, to_apply=%region_13.0 | all-reduce | flops 128 | bytes 1024 | tf_op jit(solution)/shard_map/psum | solution.py:80
  594.6 3.3 collective-permute-start.17
  599.3 4.6 collective-permute-start.21
  609.4 3.6 collective-permute-done.20
  613.4 99.8 %psum.70 = f32[128]{0:T(128)S(1)} all-reduce(f32[128]{0:T(128)S(1)} %fusion.85), channel_id=1, replica_groups=mesh['gx'=32,'gy'=8,'phys'=2] {'gx','gy','phys'}, use_global_device_ids=true, to_apply=%region_15.0 | all-reduce | flops 128 | bytes 1024 | tf_op jit(solution)/shard_map/psum | solution.py:72
  714.1 7.7 %psum.71 = f32[256]{0:T(256)S(1)} all-reduce(f32[256]{0:T(256)S(1)} %add.136), channel_id=1, replica_groups=mesh['gx'=32,'gy'=8,'phys'=2] {'phys'}, use_global_device_ids=true, to_apply=%region_18.0 | all-reduce | flops 256 | bytes 2048 | tf_op jit(solution)/shard_map/psum | solution.py:143
  (123 shorter events, 39.0 us)
Async XLA Ops:
  2.0 7.4 %collective-permute-start = (bf16[1,1,1,128,768]{4,3,2,1,0:T(8,128)(2,1)S(1)}, bf16[1,1,1,128,768]{4,3,2,1,0:T(8,128)(2,1)S(1)}, u32[]{:S(2)}, u32[]{:S(2)}) collective-permute-start(bf16[1,1,1,128,768]{4,3,2,1,0:T(8,128)(2,1)S(1)} %get-tuple-element.11), channel_id=1, source_target_pairs={{0,16},{16,32},{32,48},{48,64},{64,80},{80,96},{96,112},{112,128},... | collective-permute-start | bytes 589832 | tf_op jit(solution)/shard_map/ppermute | solution.py:17
  6.8 7.0 collective-permute-start.2
  13.9 22.2 %collective-permute-start.3 = (bf16[3,1,1,128,768]{4,3,2,1,0:T(8,128)(2,1)S(1)}, bf16[3,1,1,128,768]{4,3,2,1,0:T(8,128)(2,1)}, u32[]{:S(2)}, u32[]{:S(2)}) collective-permute-start(bf16[3,1,1,128,768]{4,3,2,1,0:T(8,128)(2,1)S(1)} %pad_maximum_fusion), channel_id=1, source_target_pairs={{0,2},{2,4},{4,6},{6,8},{8,10},{10,12},{12,14},{1,3},{3,5},{5,7},{... | collective-permute-start | bytes 1769480 | tf_op jit(solution)/shard_map/ppermute | solution.py:17
  19.8 16.3 %collective-permute-start.5 = (bf16[3,1,1,128,768]{4,3,2,1,0:T(8,128)(2,1)S(1)}, bf16[3,1,1,128,768]{4,3,2,1,0:T(8,128)(2,1)}, u32[]{:S(2)}, u32[]{:S(2)}) collective-permute-start(bf16[3,1,1,128,768]{4,3,2,1,0:T(8,128)(2,1)S(1)} %pad_maximum_fusion), channel_id=1, source_target_pairs={{2,0},{4,2},{6,4},{8,6},{10,8},{12,10},{14,12},{3,1},{5,3},{7,5},{... | collective-permute-start | bytes 1769480 | tf_op jit(solution)/shard_map/ppermute | solution.py:18
  21.9 10.0 %collective-permute-start.4 = (f32[1024]{0:T(1024)S(1)}, f32[1024]{0:T(1024)S(1)}, u32[]{:S(2)}, u32[]{:S(2)}) collective-permute-start(f32[1024]{0:T(1024)S(1)} %pad_maximum_fusion.5), channel_id=1, source_target_pairs={{2,0},{4,2},{6,4},{8,6},{10,8},{12,10},{14,12},{3,1},{5,3},{7,5},{... | collective-permute-start | bytes 12296 | tf_op jit(solution)/shard_map/ppermute | solution.py:30
  23.8 12.3 %collective-permute-start.6 = (bf16[128,768]{1,0:T(8,128)(2,1)S(1)}, bf16[128,768]{1,0:T(8,128)(2,1)}, u32[]{:S(2)}, u32[]{:S(2)}) collective-permute-start(bf16[128,768]{1,0:T(8,128)(2,1)S(1)} %get-tuple-element.12), channel_id=1, source_target_pairs={{0,1},{1,0},{2,3},{3,2},{4,5},{5,4},{6,7},{7,6},{8,9},{9,8},{10,11... | collective-permute-start | bytes 589832 | tf_op jit(solution)/shard_map/ppermute | solution.py:24
  30.4 5.4 collective-permute-start.1
  31.9 215.2 %copy-start.7 = (f32[1024]{0:T(1024)}, f32[1024]{0:T(1024)S(1)}, u32[]{:S(2)}) copy-start(f32[1024]{0:T(1024)S(1)} %collective-permute-done.4) | copy-start | bytes 12292
  240.8 6.3 collective-permute-start.7
  243.5 7.3 %collective-permute-start.8 = (bf16[1,1,1,128,768]{4,3,2,1,0:T(8,128)(2,1)S(1)}, bf16[1,1,1,128,768]{4,3,2,1,0:T(8,128)(2,1)S(1)}, u32[]{:S(2)}, u32[]{:S(2)}) collective-permute-start(bf16[1,1,1,128,768]{4,3,2,1,0:T(8,128)(2,1)S(1)} %bitcast.187), channel_id=1, source_target_pairs={{16,0},{32,16},{48,32},{64,48},{80,64},{96,80},{112,96},{128,112},... | collective-permute-start | bytes 589832 | tf_op jit(solution)/shard_map/ppermute | solution.py:18
  250.9 23.0 %collective-permute-start.10 = (bf16[3,1,1,128,768]{4,3,2,1,0:T(8,128)(2,1)S(1)}, bf16[3,1,1,128,768]{4,3,2,1,0:T(8,128)(2,1)}, u32[]{:S(2)}, u32[]{:S(2)}) collective-permute-start(bf16[3,1,1,128,768]{4,3,2,1,0:T(8,128)(2,1)S(1)} %pad_maximum_fusion.1), channel_id=1, source_target_pairs={{2,0},{4,2},{6,4},{8,6},{10,8},{12,10},{14,12},{3,1},{5,3},{7,5},{... | collective-permute-start | bytes 1769480 | tf_op jit(solution)/shard_map/ppermute | solution.py:18
  254.7 19.2 %collective-permute-start.9 = (bf16[3,1,1,128,768]{4,3,2,1,0:T(8,128)(2,1)S(1)}, bf16[3,1,1,128,768]{4,3,2,1,0:T(8,128)(2,1)}, u32[]{:S(2)}, u32[]{:S(2)}) collective-permute-start(bf16[3,1,1,128,768]{4,3,2,1,0:T(8,128)(2,1)S(1)} %pad_maximum_fusion.1), channel_id=1, source_target_pairs={{0,2},{2,4},{4,6},{6,8},{8,10},{10,12},{12,14},{1,3},{3,5},{5,7},{... | collective-permute-start | bytes 1769480 | tf_op jit(solution)/shard_map/ppermute | solution.py:17
  256.7 17.3 %collective-permute-start.11 = (bf16[128,768]{1,0:T(8,128)(2,1)S(1)}, bf16[128,768]{1,0:T(8,128)(2,1)}, u32[]{:S(2)}, u32[]{:S(2)}) collective-permute-start(bf16[128,768]{1,0:T(8,128)(2,1)S(1)} %fusion.48), channel_id=1, source_target_pairs={{0,1},{1,0},{2,3},{3,2},{4,5},{5,4},{6,7},{7,6},{8,9},{9,8},{10,11... | collective-permute-start | bytes 589832 | tf_op jit(solution)/shard_map/ppermute | solution.py:24
  374.7 233.7 %copy-start.3 = (bf16[1,1,1,768,256]{4,3,2,1,0:T(8,128)(2,1)S(1)}, bf16[1,1,1,768,256]{4,3,2,1,0:T(8,128)(2,1)}, u32[]{:S(2)}) copy-start(bf16[1,1,1,768,256]{4,3,2,1,0:T(8,128)(2,1)} %param.31) | copy-start | bytes 1179652
  374.7 4.7 collective-permute-start.12
  378.1 5.0 collective-permute-start.13
  383.1 14.9 %collective-permute-start.14 = (bf16[3,1,1,128,256]{4,3,2,1,0:T(8,128)(2,1)S(1)}, bf16[3,1,1,128,256]{4,3,2,1,0:T(8,128)(2,1)S(1)}, u32[]{:S(2)}, u32[]{:S(2)}) collective-permute-start(bf16[3,1,1,128,256]{4,3,2,1,0:T(8,128)(2,1)S(1)} %pad_maximum_fusion.2), channel_id=1, source_target_pairs={{0,2},{2,4},{4,6},{6,8},{8,10},{10,12},{12,14},{1,3},{3,5},{5,7},{... | collective-permute-start | bytes 589832 | tf_op jit(solution)/shard_map/ppermute | solution.py:17
  386.1 12.0 %collective-permute-start.15 = (bf16[3,1,1,128,256]{4,3,2,1,0:T(8,128)(2,1)S(1)}, bf16[3,1,1,128,256]{4,3,2,1,0:T(8,128)(2,1)S(1)}, u32[]{:S(2)}, u32[]{:S(2)}) collective-permute-start(bf16[3,1,1,128,256]{4,3,2,1,0:T(8,128)(2,1)S(1)} %pad_maximum_fusion.2), channel_id=1, source_target_pairs={{2,0},{4,2},{6,4},{8,6},{10,8},{12,10},{14,12},{3,1},{5,3},{7,5},{... | collective-permute-start | bytes 589832 | tf_op jit(solution)/shard_map/ppermute | solution.py:18
  388.5 9.6 %collective-permute-start.16 = (bf16[128,256]{1,0:T(8,128)(2,1)S(1)}, bf16[128,256]{1,0:T(8,128)(2,1)S(1)}, u32[]{:S(2)}, u32[]{:S(2)}) collective-permute-start(bf16[128,256]{1,0:T(8,128)(2,1)S(1)} %get-tuple-element.14), channel_id=1, source_target_pairs={{0,1},{1,0},{2,3},{3,2},{4,5},{5,4},{6,7},{7,6},{8,9},{9,8},{10,11... | collective-permute-start | bytes 196616 | tf_op jit(solution)/shard_map/ppermute | solution.py:24
  594.6 9.3 %collective-permute-start.17 = (bf16[1,1,1,128,256]{4,3,2,1,0:T(8,128)(2,1)S(1)}, bf16[1,1,1,128,256]{4,3,2,1,0:T(8,128)(2,1)S(1)}, u32[]{:S(2)}, u32[]{:S(2)}) collective-permute-start(bf16[1,1,1,128,256]{4,3,2,1,0:T(8,128)(2,1)S(1)} %bitcast.190), channel_id=1, source_target_pairs={{0,16},{16,32},{32,48},{48,64},{64,80},{80,96},{96,112},{112,128},... | collective-permute-start | bytes 196616 | tf_op jit(solution)/shard_map/ppermute | solution.py:17
  597.9 6.0 collective-permute-start.18
  599.3 9.2 %collective-permute-start.21 = (bf16[128,256]{1,0:T(8,128)(2,1)S(1)}, bf16[128,256]{1,0:T(8,128)(2,1)S(1)}, u32[]{:S(2)}, u32[]{:S(2)}) collective-permute-start(bf16[128,256]{1,0:T(8,128)(2,1)S(1)} %fusion.86), channel_id=1, source_target_pairs={{0,1},{1,0},{2,3},{3,2},{4,5},{5,4},{6,7},{7,6},{8,9},{9,8},{10,11... | collective-permute-start | bytes 196616 | tf_op jit(solution)/shard_map/ppermute | solution.py:24
  603.9 5.5 collective-permute-start.19
  606.0 7.0 collective-permute-start.20
  (27 other events, 1891.7 us)
where the time goes:
time: 724 us; the launch traced here: 723 us
  blocking collectives  603 us (83%)
  starting transfers between devices  66.2 us (9%)
  waiting for transfers between devices  39.9 us (6%)
    psum x2, blocking collectives, interface_solve(): current = lax.psum(jnp.sum(load * load, axis=1), ('gx', 'gy', 'phys'))  207 us
    psum x2, blocking collectives, interface_solve(): curvature = lax.psum(local_curv, ('gx', 'gy', 'phys'))  198 us
    psum x2, blocking collectives, interface_solve(): lax.psum(jnp.sum(residual * residual, axis=1), ('gx', 'gy', 'phys'))  190 us
    ppermute x8, starting transfers between devices, with_halo(): before = lax.ppermute(last, axis, up)  27.1 us
    ppermute x4, starting transfers between devices, from_partner(): lax.ppermute(array, axis, [(i, i ^ 1 << apart) for i in range(lax.axis_si...  20.2 us
    ppermute x4, waiting for transfers between devices, from_partner(): lax.ppermute(array, axis, [(i, i ^ 1 << apart) for i in range(lax.axis_si...  16 us
    ppermute x8, starting transfers between devices, with_halo(): after = lax.ppermute(initial, axis, down)  15.7 us
    ppermute x8, waiting for transfers between devices, with_halo(): after = lax.ppermute(initial, axis, down)  15.5 us
  transfers between devices with their start and end apart: 22, of which 11 were waited for; matrix products, arithmetic and copies ran while one was open for 0% of the time, Pallas kernels for 0%

commit v1 on v0

v1 whole, which is shorter than its diff:
```python
import functools

import jax
import jax.numpy as jnp
from jax import lax
from jax.experimental import pallas as pl
from jax.experimental.pallas import tpu as pltpu
from jax.sharding import PartitionSpec as P

MESH = pl.DeviceIdType.MESH
F32 = jnp.float32
BF16 = jnp.bfloat16
ROWS = 16
LOADS = 128
HALF = LOADS // 2


def ring(k, n):
    return min(k, n - k)


def remote(src, dst, send, recv, peer):
    return pltpu.make_async_remote_copy(
        src_ref=src, dst_ref=dst, send_sem=send, recv_sem=recv, device_id=peer, device_id_type=MESH
    )


def row_loop(body):
    def step(n, carry):
        body(pl.ds(pl.multiple_of(n * ROWS, ROWS), ROWS))
        return carry

    lax.fori_loop(0, LOADS // ROWS, step, 0)


def lanes(x):
    return jnp.sum(x, axis=1, keepdims=True)


def times(a, b):
    return jnp.dot(a, b, preferred_element_type=F32)


def times_t(a, b):
    return lax.dot_general(a, b, (((1,), (1,)), ((), ())), preferred_element_type=F32)


def step_sizes(total):
    rr, rw, ww, gw, hw = (total[k : k + 1, :] for k in range(5))
    alpha = rr / rw
    beta = (rr - 2.0 * alpha * rw + alpha * alpha * ww) / rr
    grow = 1.0 + beta
    curve = grow * grow * rw - 2.0 * grow * alpha * gw + alpha * alpha * hw
    second = beta * rr / curve
    return alpha + second * grow, -second * alpha


def kernel(
    nx, ny, xs, zs,
    ml, hl, mf, hf, md, hd, mx, my, mp, hx, hy, hp, cp, ms, hs, dn, ids, scale,
    out_m, out_h, out_g,
    r0, h0, zf, bf, mw, hw, mup, hup, cf, sm, sh, den, mat,
    q0, qn, w0, wb, wn, hu, hun, uf, bhu, vf, vb, vn, bv, s0, bs, bsb, bsn,
    msc, col, mom, arx1, ary1, arx2, ary2, xm, xh, sp, sr,
    lsem, osem, wsend, wrecv, esend, erecv, asend, arecv, fsem,
):
    i, j, f = lax.axis_index("gx"), lax.axis_index("gy"), lax.axis_index("phys")
    low_x, high_x, low_y, high_y = i > 0, i < nx - 1, j > 0, j < ny - 1
    up_x = (jnp.minimum(i + 1, nx - 1), j, f)
    down_x = (jnp.maximum(i - 1, 0), j, f)
    up_y = (i, jnp.minimum(j + 1, ny - 1), f)
    down_y = (i, jnp.maximum(j - 1, 0), f)
    other = (i, j, 1 - f)
    target = (up_x, down_x, up_y, down_y, other)
    sends = (high_x, low_x, high_y, low_y, None)
    gets = (low_x, high_x, low_y, high_y, None)

    def guarded(cond, fn):
        if cond is None:
            fn()
        else:
            pl.when(cond)(fn)

    xi, zi = lax.div(i, zs), lax.rem(i, zs)
    offsets = [(a, b) for a in range(xs) for b in range(zs) if (a, b) != (0, 0)]
    offsets.sort(key=lambda o: -(ring(o[0], xs) + ring(o[1], zs)))
    x_peers = [(lax.rem(xi + a, xs) * zs + lax.rem(zi + b, zs), j, f) for a, b in offsets]
    n_yp = ny * 2
    yi, ci = f * (ny // 2) + lax.div(j, 2), lax.rem(j, 2)
    offsets = [(a, b) for a in range(ny) for b in range(2) if (a, b) != (0, 0)]
    offsets.sort(key=lambda o: -(ring(o[0], ny) + 0.1 * o[1]))
    y_peers = []
    for a, b in offsets:
        y = lax.rem(yi + a, ny)
        y_peers.append((i, lax.rem(y, ny // 2) * 2 + lax.rem(ci + b, 2), lax.div(y, ny // 2)))
    x_slot, y_slot = i, yi * 2 + ci

    loads = []

    def load(src, dst):
        copy = pltpu.make_async_copy(src, dst, lsem.at[len(loads)])
        copy.start()
        loads.append(copy)
        return copy

    get_r0 = load(ml.at[0, 0, 0], r0)
    small = [
        load(md.at[0, 0], mw.at[0]), load(mx.at[0, 0], mw.at[1]), load(my.at[0, 0], mw.at[2]),
        load(mp.at[0], mw.at[3]),
        load(hd.at[0, 0], hw.at[0]), load(hx.at[0, 0], hw.at[1]), load(hy.at[0, 0], hw.at[2]),
        load(hp.at[0], hw.at[3]),
    ]
    get_z = load(mf.at[0, 0, 0], zf)
    get_c = load(cp.at[0, 0, 0], cf)
    get_h = load(hl.at[0, 0, 0], h0)
    get_b = load(hf.at[0, 0, 0], bf)
    late = [
        load(ms.at[0, 0, 0], sm), load(hs.at[0, 0, 0], sh),
        load(dn.at[0], den), load(ids.at[0], mat),
    ]

    barrier = pltpu.get_barrier_semaphore()
    for peer in y_peers + x_peers:
        pl.semaphore_signal(barrier, inc=1, device_id=peer, device_id_type=MESH)

    for d, there in enumerate(gets[:4]):
        @pl.when(jnp.logical_not(there))
        def _():
            qn[d] = jnp.zeros_like(qn[d])
            wn[d] = jnp.zeros_like(wn[d])
            hun[d] = jnp.zeros_like(hun[d])
            vn[d] = jnp.zeros_like(vn[d])
            bsn[d] = jnp.zeros_like(bsn[d])
    for d, there in ((0, high_x), (1, high_y)):
        @pl.when(jnp.logical_not(there))
        def _():
            mup[d] = jnp.zeros_like(mup[d])
            hup[d] = jnp.zeros_like(hup[d])
    col[...] = jnp.zeros_like(col)
    msc[...] = jnp.zeros_like(msc)

    def exchange(stage, src_of, dst):
        def copy(d):
            k = stage * 5 + d
            return remote(src_of(d), dst.at[d], esend.at[k], erecv.at[k], target[d])

        def start(order=(4, 0, 1, 2, 3)):
            for d in order:
                guarded(sends[d], lambda: copy(d).start())

        def arrive(order=(0, 1, 2, 3)):
            for d in order:
                guarded(gets[d], lambda: copy(d).wait_recv())

        def sent(order=(0, 1, 2, 3, 4)):
            for d in order:
                guarded(sends[d], lambda: copy(d).wait_send())

        return start, arrive, sent

    low, high = pl.ds(0, HALF), pl.ds(HALF, HALF)
    mine = pl.ds(pl.multiple_of(f * HALF, HALF), HALF)
    yours = pl.ds(pl.multiple_of((1 - f) * HALF, HALF), HALF)
    half = (low, high, low, high, yours)
    q_start, q_arrive, q_sent = exchange(0, lambda d: q0, qn)
    hu_start, hu_arrive, hu_sent = exchange(1, lambda d: hu, hun)
    w_start, w_arrive, w_sent = exchange(2, lambda d: wb.at[half[d]], wn)
    v_start, v_arrive, v_sent = exchange(3, lambda d: vb, vn)
    b_start, b_arrive, b_sent = exchange(4, lambda d: bsb.at[half[d]], bsn)

    get_r0.wait()
    q0[...] = r0[...].astype(BF16)
    pl.semaphore_wait(barrier, len(x_peers) + len(y_peers))
    q_start()
    for copy in small:
        copy.wait()

    def weights(k):
        src, dst, peer = (
            (mw.at[1], mup.at[0], down_x), (mw.at[2], mup.at[1], down_y),
            (hw.at[1], hup.at[0], down_x), (hw.at[2], hup.at[1], down_y),
        )[k]
        return remote(src, dst, wsend.at[k], wrecv.at[k], peer)

    for k in range(4):
        guarded((low_x, low_y)[k % 2], lambda: weights(k).start())

    get_z.wait()
    inner = times(q0[...], zf[...]).astype(BF16)
    w0[...] = times_t(inner, zf[...])
    get_c.wait()
    uf[...] = times(q0[...], cf[...])
    get_h.wait()
    hu[:, :256] = h0[...].astype(BF16)
    hu[:, 256:] = uf[...].astype(BF16)
    get_b.wait()
    for n in range(2):
        cols = slice(256 * n, 256 * n + 256)
        inner = times(hu[:, cols], bf[...]).astype(BF16)
        bhu[:, cols] = times_t(inner, bf[...])
    for k in range(4):
        guarded((high_x, high_y)[k % 2], lambda: weights(k).wait_recv())

    def near(part, w, up, values, nb, rows, cols=slice(None)):
        diag, wx, wy, wp = w[0], w[1], w[2], w[3]
        ux, uy = up[0], up[1]
        total = part + (diag + wx + ux + wy + uy + wp) * values
        total = total - wx * nb[0, rows, cols].astype(F32) - ux * nb[1, rows, cols].astype(F32)
        return total - wy * nb[2, rows, cols].astype(F32) - uy * nb[3, rows, cols].astype(F32)

    q_arrive()

    def body(rows):
        w0[rows, :] = near(w0[rows, :], mw, mup, q0[rows, :].astype(F32), qn, rows)

    row_loop(body)
    q_sent((4,))
    hu_start()
    q_arrive((4,))

    def body(rows):
        w = w0[rows, :] - mw[3] * qn[4, rows, :].astype(F32)
        w0[rows, :] = w
        wb[rows, :] = w.astype(BF16)

    row_loop(body)
    w_start()
    vf[...] = times(wb[...], cf[...])
    vb[...] = vf[...].astype(BF16)
    v_start()

    def moments(r, w, b, first, edge, inner, weight, up):
        def body(rows):
            rv, wv, bv_ = r[rows, :], w[rows, :], b[rows, :].astype(F32)
            col[rows, 0:1] = lanes(rv * rv)
            col[rows, 1:2] = lanes(rv * wv)
            col[rows, 2:3] = lanes(wv * wv)
            col[rows, 3:4] = lanes(bv_ * wv)
            col[rows, 4:5] = lanes(weight[0] * bv_ * bv_) + lanes(inner[rows, :] * inner[rows, :])

        row_loop(body)

    def edges(b, nb, weight, up):
        ends = jnp.where(low_x, 0.0, weight[1]) + jnp.where(low_y, 0.0, weight[2])

        def body(n, carry):
            rows = pl.ds(pl.multiple_of(n * ROWS, ROWS), ROWS)
            bv_ = b[rows, :].astype(F32)
            dx, dy = bv_ - nb[0, rows, :].astype(F32), bv_ - nb[2, rows, :].astype(F32)
            col[rows, 4:5] += lanes(weight[1] * dx * dx + weight[2] * dy * dy)
            upper = pl.ds(pl.multiple_of(HALF + n * ROWS, ROWS), ROWS)
            bv_ = b[upper, :].astype(F32)
            dx, dy = bv_ - nb[1, rows, :].astype(F32), bv_ - nb[3, rows, :].astype(F32)
            col[upper, 4:5] += lanes(up[0] * dx * dx + up[1] * dy * dy + ends * bv_ * bv_)
            return carry

        lax.fori_loop(0, HALF // ROWS, body, 0)

    def face_edges(b, nb, weight):
        def body(n, carry):
            rows = pl.ds(pl.multiple_of(n * ROWS, ROWS), ROWS)
            own = pl.ds(pl.multiple_of(f * HALF + n * ROWS, ROWS), ROWS)
            d = b[own, :].astype(F32) - nb[4, rows, :].astype(F32)
            col[own, 4:5] += lanes(weight[3] * d * d)
            return carry

        lax.fori_loop(0, HALF // ROWS, body, 0)

    def sum_start(buf, slot, peers, k):
        for peer in peers:
            remote(mom.at[k], buf.at[slot], asend.at[k], arecv.at[k], peer).start()
        buf[slot] = mom[k]

    def sum_end(buf, k):
        rest = buf.at[pl.ds(0, buf.shape[0] - 1)]
        pltpu.make_async_copy(rest, rest, arecv.at[k]).wait()
        return jnp.sum(buf[...], axis=0)

    def sum_sent(buf, k):
        rest = buf.at[pl.ds(0, buf.shape[0] - 1)]
        pltpu.make_async_copy(rest, rest, asend.at[k]).wait()

    xm[...] = times(wb[...], zf[...])
    moments(r0, w0, wb, None, None, xm, mw, mup)
    w_arrive()
    edges(wb, wn, mw, mup)
    w_arrive((4,))
    face_edges(wb, wn, mw)
    mom[0] = jnp.transpose(col[...])[:8, :]
    sum_start(arx1, x_slot, x_peers, 0)

    hu_arrive((0, 1, 2, 3, 4))

    def body(rows):
        for n in range(2):
            cols = slice(256 * n, 256 * n + 256)
            near_part = near(
                bhu[rows, cols], hw, hup, hu[rows, cols].astype(F32), hun, rows, cols
            )
            bhu[rows, cols] = near_part - hw[3] * hun[4, rows, cols].astype(F32)

    row_loop(body)
    mom[1] = sum_end(arx1, 0)
    sum_start(ary1, y_slot, y_peers, 1)
    inner = times(vb[...], bf[...]).astype(BF16)
    bv[...] = times_t(inner, bf[...])
    v_arrive((0, 1, 2, 3, 4))

    def body(rows):
        near_part = near(bv[rows, :], hw, hup, vb[rows, :].astype(F32), vn, rows)
        bv[rows, :] = near_part - hw[3] * vn[4, rows, :].astype(F32)

    row_loop(body)

    def columns(pair, k):
        msc[0:1, :] = pair[0]
        msc[1:2, :] = pair[1]
        col[...] = jnp.transpose(msc[...])

    total = sum_end(ary1, 1)
    columns(step_sizes(total), 0)

    def body(rows):
        a, b = col[rows, 0:1], col[rows, 1:2]
        s0[rows, :] = h0[rows, :] - a * uf[rows, :] - b * vf[rows, :]
        image = bhu[rows, :256] - a * bhu[rows, 256:] - b * bv[rows, :]
        bs[rows, :] = image
        bsb[rows, :] = image.astype(BF16)

    row_loop(body)
    b_start()

    def body(n, energy):
        rows = pl.ds(pl.multiple_of(n * ROWS, ROWS), ROWS)
        x = col[rows, 0:1] * r0[rows, :] + col[rows, 1:2] * w0[rows, :]
        xm[rows, :] = x
        return energy + jnp.sum(x * x, axis=0, keepdims=True)

    m_energy = lax.fori_loop(0, LOADS // ROWS, body, jnp.zeros((1, r0.shape[1]), F32))
    put_m = pltpu.make_async_copy(xm, out_m.at[0, 0, 0], osem.at[0])
    put_m.start()

    xh[...] = times(bsb[...], bf[...])
    moments(s0, bs, bsb, None, None, xh, hw, hup)
    b_arrive()
    edges(bsb, bsn, hw, hup)
    b_arrive((4,))
    face_edges(bsb, bsn, hw)
    mom[2] = jnp.transpose(col[...])[:8, :]
    sum_start(arx2, x_slot, x_peers, 2)
    for copy in late:
        copy.wait()
    wide = jnp.broadcast_to(m_energy.astype(BF16), (16, m_energy.shape[1]))
    sens = times(wide, sm[...])
    mom[3] = sum_end(arx2, 2)
    sum_start(ary2, y_slot, y_peers, 3)
    total = sum_end(ary2, 3)
    columns(step_sizes(total), 1)

    def body(n, energy):
        rows = pl.ds(pl.multiple_of(n * ROWS, ROWS), ROWS)
        x = col[rows, 0:1] * s0[rows, :] + col[rows, 1:2] * bs[rows, :]
        xh[rows, :] = x
        return energy + jnp.sum(x * x, axis=0, keepdims=True)

    h_energy = lax.fori_loop(0, LOADS // ROWS, body, jnp.zeros((1, h0.shape[1]), F32))
    put_h = pltpu.make_async_copy(xh, out_h.at[0, 0, 0], osem.at[1])
    put_h.start()
    wide = jnp.broadcast_to(h_energy.astype(BF16), (16, h_energy.shape[1]))
    sens = sens + times(wide, sh[...])
    sp[0] = sens[:8, :128]
    sp[1] = sens[:8, 128:]
    swap = remote(sp.at[1 - f], sr, fsem.at[0], fsem.at[1], other)
    swap.start()
    kinds = mat[...]
    stiffness = jnp.zeros(kinds.shape, F32)
    for k in range(scale.shape[0]):
        stiffness = jnp.where(kinds == k, scale[k], stiffness)
    factor = -3.0 * den[...] * den[...] * stiffness / LOADS
    swap.wait()
    out_g[0] = factor * (sp[f, 0:1, :] + sr[0:1, :])

    for k in range(4):
        guarded((low_x, low_y)[k % 2], lambda: weights(k).wait_send())
    q_sent((0, 1, 2, 3))
    for sent in (hu_sent, w_sent, v_sent, b_sent):
        sent()
    for k, buf in enumerate((arx1, ary1, arx2, ary2)):
        sum_sent(buf, k)
    put_m.wait()
    put_h.wait()


def solution(mesh):
    nx, ny = mesh.shape["gx"], mesh.shape["gy"]
    zs = 8 if nx % 8 == 0 else 1
    xs = nx // zs

    def vm(*shape, dtype=F32):
        return pltpu.VMEM(shape, dtype)

    def bm(*shape):
        return pltpu.VMEM(shape, BF16)

    any_spec = pl.BlockSpec(memory_space=pltpu.HBM)
    sems = pltpu.SemaphoreType.DMA

    def on_device(*args):
        return pl.pallas_call(
            functools.partial(kernel, nx, ny, xs, zs),
            out_shape=(
                jax.ShapeDtypeStruct((1, 1, 1, 128, 768), F32),
                jax.ShapeDtypeStruct((1, 1, 1, 128, 256), F32),
                jax.ShapeDtypeStruct((1, 1, 128), F32),
            ),
            in_specs=[any_spec] * 17 + [pl.BlockSpec(memory_space=pltpu.SMEM)],
            out_specs=(any_spec, any_spec, pl.BlockSpec(memory_space=pltpu.VMEM)),
            scratch_shapes=[
                vm(128, 768), vm(128, 256), bm(768, 768), bm(256, 256),
                vm(4, 1, 768), vm(4, 1, 256), vm(2, 1, 768), vm(2, 1, 256),
                bm(768, 256), bm(768, 256), bm(256, 256), vm(1, 128), vm(1, 128, dtype=jnp.int32),
                bm(128, 768), bm(5, 128, 768), vm(128, 768), bm(128, 768), bm(5, 64, 768),
                bm(128, 512), bm(5, 128, 512), vm(128, 256), vm(128, 512),
                vm(128, 256), bm(128, 256), bm(5, 128, 256), vm(128, 256),
                vm(128, 256), vm(128, 256), bm(128, 256), bm(5, 64, 256),
                vm(128, 128), vm(128, 128), vm(4, 8, 128),
                vm(nx, 8, 128), vm(ny * 2, 8, 128), vm(nx, 8, 128), vm(ny * 2, 8, 128),
                vm(128, 768), vm(128, 256), vm(2, 8, 128), vm(8, 128),
                sems((17,)), sems((2,)), sems((4,)), sems((4,)), sems((25,)), sems((25,)),
                sems((4,)), sems((4,)), sems((2,)),
            ],
            compiler_params=pltpu.CompilerParams(
                collective_id=0, has_side_effects=True, vmem_limit_bytes=32 * 1024 * 1024
            ),
        )(*args)

    block = P("gx", "gy", "phys", None, None)
    line = P("gx", "gy", "phys", None)
    both = P("gx", "gy", None)
    part = P("gx", "gy", "phys")
    return jax.shard_map(
        on_device,
        mesh=mesh,
        in_specs=(
            block, block, block, block, line, line, line, line, both, line, line, both,
            block, block, block, part, part, P(),
        ),
        out_specs=(block, block, part),
        check_vma=False,
    )
```

time: 724 us -> 97.8 us (0.14)
  blocking collectives: 603 us -> 0 us
  Pallas kernels: 0 us -> 80.3 us
  starting transfers between devices: 66.2 us -> 0 us
  waiting for transfers between devices: 39.9 us -> 0 us
  local copies, waits for them, and re-layouts: 1.54 us -> 16.3 us
    psum x7 -> x0, blocking collectives: 603 us -> none  [the longest x2 207 us: interface_solve(): current = lax.psum(jnp.sum(load * load, axis=1), ('gx', 'gy', 'phys'))]
    pallas_call x0 -> x1, Pallas kernels: none -> 80.3 us  [on_device(): pl.pallas_call(functools.partial(kernel, nx, ny, xs, zs), out_shape=(jax....]
    ppermute x22 -> x0, starting transfers between devices: 66.2 us -> none  [the longest x8 27.1 us: with_halo(): before = lax.ppermute(last, axis, up)]
    ppermute x22 -> x0, waiting for transfers between devices: 39.9 us -> none  [the longest x4 16 us: from_partner(): lax.ppermute(array, axis, [(i, i ^ 1 << apart) for i in range(lax.axis_si...]
    unnamed x58 -> x39, local copies, waits for them, and re-layouts: 0.16 us -> 16.3 us
  transfers between devices with their start and end apart: 22 -> 0, of which waited for: 11 -> 0; matrix products, arithmetic and copies ran while one was open for 0% -> 0% of each run, Pallas kernels for 0% -> 0%
where the time goes in v1:
time: 97.8 us; the launch traced here: 97.3 us
  Pallas kernels  80.3 us (82%)
  local copies, waits for them, and re-layouts  16.3 us (17%)
    pallas_call x1, Pallas kernels, on_device(): pl.pallas_call(functools.partial(kernel, nx, ny, xs, zs), out_shape=(jax....  80.3 us
    unnamed x39, local copies, waits for them, and re-layouts  16.3 us

profile of v1, /device:TPU:1, one launch (start us, length us, event | category | flops | bytes accessed | tf_op | source)
XLA Modules:
  0.0 97.3 jit_solution(5438286487737600090)
XLA Ops:
  0.6 0.0 copy-start
  0.6 1.3 %copy-done = bf16[1,1,1,768,768]{4,3,2,1,0:T(8,128)(2,1)S(1)} copy-done((bf16[1,1,1,768,768]{4,3,2,1,0:T(8,128)(2,1)S(1)}, bf16[1,1,1,768,768]{4,3,2,1,0:T(8,128)(2,1)}, u32[]{:S(2)}) %copy-start) | copy-done | bytes 1179672
  1.9 0.0 copy-start.1
  1.9 1.0 %copy-done.1 = f32[1,1,1,128,768]{4,3,2,1,0:T(8,128)S(1)} copy-done((f32[1,1,1,128,768]{4,3,2,1,0:T(8,128)S(1)}, f32[1,1,1,128,768]{4,3,2,1,0:T(8,128)}, u32[]{:S(2)}) %copy-start.1) | copy-done | bytes 393240
  2.9 1.0 %copy-done.2 = bf16[1,1,1,768,256]{4,3,2,1,0:T(8,128)(2,1)S(1)} copy-done((bf16[1,1,1,768,256]{4,3,2,1,0:T(8,128)(2,1)S(1)}, bf16[1,1,1,768,256]{4,3,2,1,0:T(8,128)(2,1)}, u32[]{:S(2)}) %copy-start.2) | copy-done | bytes 393240
  3.9 1.0 %copy-done.3 = bf16[1,1,1,768,256]{4,3,2,1,0:T(8,128)(2,1)S(1)} copy-done((bf16[1,1,1,768,256]{4,3,2,1,0:T(8,128)(2,1)S(1)}, bf16[1,1,1,768,256]{4,3,2,1,0:T(8,128)(2,1)}, u32[]{:S(2)}) %copy-start.3) | copy-done | bytes 393240
  4.9 0.9 copy-done.4
  5.8 0.9 copy-done.5
  6.7 0.9 copy-done.6
  7.6 0.7 copy-done.7
  8.3 0.7 copy-done.8
  9.0 0.7 copy-done.9
  9.7 0.7 copy-done.10
  10.4 0.7 copy-done.11
  11.0 0.7 copy-done.12
  11.7 0.7 copy-done.13
  12.4 0.7 copy-done.14
  13.1 0.7 copy-done.15
  13.7 0.7 copy-done.16
  14.4 0.7 copy-done.17
  15.0 80.3 %shard_map.193 = (f32[1,1,1,128,768]{4,3,2,1,0:T(8,128)S(1)}, f32[1,1,1,128,256]{4,3,2,1,0:T(8,128)S(1)}, f32[1,1,128]{2,1,0:T(1,128)S(1)}) custom-call(f32[1,1,1,128,768]{4,3,2,1,0:T(8,128)S(1)} %copy-done.1, f32[1,1,1,128,256]{4,3,2,1,0:T(8,128)S(1)} %copy-done.4, bf16[1,1,1,768,768]{4,3,2,1,0:T(8,128)(2,1)S(1)} %copy-done, ...), custom_call_target="tpu_custom_call" | custom-call | tf_op jit(solution)/shard_map/pallas_call | solution.py:409
  95.4 0.7 copy.24
  96.1 0.7 copy.25
  96.8 0.5 copy.26
  (16 shorter events, 0.0 us)
Async XLA Ops:
  0.6 1.3 %copy-start = (bf16[1,1,1,768,768]{4,3,2,1,0:T(8,128)(2,1)S(1)}, bf16[1,1,1,768,768]{4,3,2,1,0:T(8,128)(2,1)}, u32[]{:S(2)}) copy-start(bf16[1,1,1,768,768]{4,3,2,1,0:T(8,128)(2,1)} %mf.1) | copy-start | bytes 3538948
  1.9 1.0 %copy-start.1 = (f32[1,1,1,128,768]{4,3,2,1,0:T(8,128)S(1)}, f32[1,1,1,128,768]{4,3,2,1,0:T(8,128)}, u32[]{:S(2)}) copy-start(f32[1,1,1,128,768]{4,3,2,1,0:T(8,128)} %ml.1) | copy-start | bytes 1179652
  2.9 1.0 %copy-start.2 = (bf16[1,1,1,768,256]{4,3,2,1,0:T(8,128)(2,1)S(1)}, bf16[1,1,1,768,256]{4,3,2,1,0:T(8,128)(2,1)}, u32[]{:S(2)}) copy-start(bf16[1,1,1,768,256]{4,3,2,1,0:T(8,128)(2,1)} %cp.1) | copy-start | bytes 1179652
  3.9 1.0 %copy-start.3 = (bf16[1,1,1,768,256]{4,3,2,1,0:T(8,128)(2,1)S(1)}, bf16[1,1,1,768,256]{4,3,2,1,0:T(8,128)(2,1)}, u32[]{:S(2)}) copy-start(bf16[1,1,1,768,256]{4,3,2,1,0:T(8,128)(2,1)} %ms.1) | copy-start | bytes 1179652
  4.9 0.9 copy-start.4
  5.8 0.9 copy-start.5
  6.7 0.9 copy-start.6
  7.6 0.7 copy-start.7
  8.3 0.7 copy-start.8
  9.0 0.7 copy-start.9
  9.7 0.7 copy-start.10
  10.4 0.7 copy-start.11
  11.0 0.7 copy-start.12
  11.7 0.7 copy-start.13
  12.4 0.7 copy-start.14
  13.1 0.7 copy-start.15
  13.7 0.7 copy-start.16
  14.4 0.7 copy-start.17

commit v2 on v1

v2 whole, which is shorter than its diff:
```python
import functools

import jax
import jax.numpy as jnp
from jax import lax
from jax.experimental import pallas as pl
from jax.experimental.pallas import tpu as pltpu
from jax.sharding import PartitionSpec as P

MESH = pl.DeviceIdType.MESH
F32 = jnp.float32
BF16 = jnp.bfloat16
ROWS = 16
LOADS = 128
HALF = LOADS // 2


def ring(k, n):
    return min(k, n - k)


def remote(src, dst, send, recv, peer):
    return pltpu.make_async_remote_copy(
        src_ref=src, dst_ref=dst, send_sem=send, recv_sem=recv, device_id=peer, device_id_type=MESH
    )


class Once:
    def __init__(self, wait, group):
        self.pending = wait
        group.append(self)

    def wait(self):
        if self.pending is not None:
            self.pending()
            self.pending = None


def row_loop(body, count=LOADS):
    def step(n, carry):
        body(pl.ds(pl.multiple_of(n * ROWS, ROWS), ROWS))
        return carry

    lax.fori_loop(0, count // ROWS, step, 0)


def lanes(x):
    return jnp.sum(x, axis=1, keepdims=True)


def times(a, b):
    return jnp.dot(a, b, preferred_element_type=F32)


def times_t(a, b):
    return lax.dot_general(a, b, (((1,), (1,)), ((), ())), preferred_element_type=F32)


def step_sizes(total):
    rr, rw, ww, gw, hw = (total[k : k + 1, :] for k in range(5))
    alpha = rr / rw
    beta = (rr - 2.0 * alpha * rw + alpha * alpha * ww) / rr
    grow = 1.0 + beta
    curve = grow * grow * rw - 2.0 * grow * alpha * gw + alpha * alpha * hw
    second = beta * rr / curve
    return alpha + second * grow, -second * alpha


def kernel(
    nx, ny, xs, zs,
    ml, hl, mf, hf, md, hd, mx, my, mp, hx, hy, hp, cp, ms, hs, dn, ids, sc,
    out_m, out_h, out_g,
    r0, h0, zf, bf, mw, hw, mup, hup, cf, sm, sh, shp, den, mat, scale,
    q0, qn, w0, wb, wn, hb, hn, bh, uv, uvb, uvn, buv, s0, sp, bs, bsb, bsn, bsp,
    msc, col, mom, arx1, ary1, arx2, ary2, xm, xh, part, got,
    lsem, wsend, wrecv, esend, erecv, asend, arecv, fsend, frecv,
):
    i, j, f = lax.axis_index("gx"), lax.axis_index("gy"), lax.axis_index("phys")
    low_x, high_x, low_y, high_y = i > 0, i < nx - 1, j > 0, j < ny - 1
    up_x = (jnp.minimum(i + 1, nx - 1), j, f)
    down_x = (jnp.maximum(i - 1, 0), j, f)
    up_y = (i, jnp.minimum(j + 1, ny - 1), f)
    down_y = (i, jnp.maximum(j - 1, 0), f)
    other = (i, j, 1 - f)
    target = (up_x, down_x, up_y, down_y, other)
    sends = (high_x, low_x, high_y, low_y, None)
    gets = (low_x, high_x, low_y, high_y, None)

    def guarded(cond, fn):
        if cond is None:
            fn()
        else:
            pl.when(cond)(fn)

    xi, zi = lax.div(i, zs), lax.rem(i, zs)
    offsets = [(a, b) for a in range(xs) for b in range(zs) if (a, b) != (0, 0)]
    offsets.sort(key=lambda o: -(ring(o[0], xs) + ring(o[1], zs)))
    x_peers = [(lax.rem(xi + a, xs) * zs + lax.rem(zi + b, zs), j, f) for a, b in offsets]
    yi, ci = f * (ny // 2) + lax.div(j, 2), lax.rem(j, 2)
    offsets = [(a, b) for a in range(ny) for b in range(2) if (a, b) != (0, 0)]
    offsets.sort(key=lambda o: -(ring(o[0], ny) + 0.1 * o[1]))
    y_peers = []
    for a, b in offsets:
        y = lax.rem(yi + a, ny)
        y_peers.append((i, lax.rem(y, ny // 2) * 2 + lax.rem(ci + b, 2), lax.div(y, ny // 2)))
    x_slot, y_slot = i, yi * 2 + ci

    finish = []

    def load(src, dst):
        copy = pltpu.make_async_copy(src, dst, lsem.at[len(finish)])
        copy.start()
        return Once(copy.wait, finish)

    def close():
        for piece in finish:
            piece.wait()

    get_r0 = load(ml.at[0, 0, 0], r0)
    barrier = pltpu.get_barrier_semaphore()
    for peer in y_peers + x_peers:
        pl.semaphore_signal(barrier, inc=1, device_id=peer, device_id_type=MESH)

    for d, there in enumerate(gets[:4]):
        @pl.when(jnp.logical_not(there))
        def _():
            for ref in (qn, wn, hn, uvn, bsn):
                ref[d] = jnp.zeros_like(ref[d])
    for d, there in ((0, high_x), (1, high_y)):
        @pl.when(jnp.logical_not(there))
        def _():
            mup[d] = jnp.zeros_like(mup[d])
            hup[d] = jnp.zeros_like(hup[d])

    def exchange(stage, src_of, dst_of):
        receipts, departures = {}, {}

        def copy(d):
            k = stage * 5 + d
            return remote(src_of(d), dst_of(d), esend.at[k], erecv.at[k], target[d])

        def start(order=(4, 0, 1, 2, 3)):
            for d in order:
                guarded(sends[d], lambda: copy(d).start())
                receipts[d] = Once(lambda d=d: guarded(gets[d], copy(d).wait_recv), finish)
                departures[d] = Once(lambda d=d: guarded(sends[d], copy(d).wait_send), finish)

        def arrive(order=(0, 1, 2, 3)):
            for d in order:
                receipts[d].wait()

        def sent(order):
            for d in order:
                departures[d].wait()

        return start, arrive, sent

    low, high = pl.ds(0, HALF), pl.ds(HALF, HALF)
    mine = pl.ds(pl.multiple_of(f * HALF, HALF), HALF)
    yours = pl.ds(pl.multiple_of((1 - f) * HALF, HALF), HALF)
    half = (low, high, low, high, yours)
    q_start, q_arrive, q_sent = exchange(0, lambda d: q0, lambda d: qn.at[d])
    h_start, h_arrive, h_sent = exchange(1, lambda d: hb, lambda d: hn.at[d])
    w_start, w_arrive, w_sent = exchange(2, lambda d: wb.at[half[d]], lambda d: wn.at[d])
    uv_start, uv_arrive, uv_sent = exchange(3, lambda d: uvb, lambda d: uvn.at[d])
    b_start, b_arrive, b_sent = exchange(
        4, lambda d: bsb.at[half[d]], lambda d: bsp.at[yours] if d == 4 else bsn.at[d]
    )

    def face_send(k, src, dst):
        copy = remote(src, dst, fsend.at[k], frecv.at[k], other)
        copy.start()
        Once(copy.wait_send, finish)
        return Once(copy.wait_recv, finish)

    get_r0.wait()
    q0[...] = r0[...].astype(BF16)
    pl.semaphore_wait(barrier, len(x_peers) + len(y_peers))
    q_start()
    small = [
        load(md.at[0, 0], mw.at[0]), load(mx.at[0, 0], mw.at[1]), load(my.at[0, 0], mw.at[2]),
        load(mp.at[0], mw.at[3]),
        load(hd.at[0, 0], hw.at[0]), load(hx.at[0, 0], hw.at[1]), load(hy.at[0, 0], hw.at[2]),
        load(hp.at[0], hw.at[3]),
    ]
    get_z = load(mf.at[0, 0, 0], zf)
    get_c = load(cp.at[0, 0, 0], cf)
    get_h = load(hl.at[0, 0, 0], h0)
    get_b = load(hf.at[0, 0, 0], bf)
    get_sm = load(ms.at[0, 0, 0], sm)
    get_sh = [load(hs.at[0, 0, 0, :, pl.ds(128 * k, 128)], sh.at[k]) for k in range(2)]
    get_last = [load(dn.at[0], den), load(ids.at[0], mat), load(sc, scale)]
    for copy in small:
        copy.wait()

    def weights(k):
        src, dst, peer = (
            (mw.at[1], mup.at[0], down_x), (mw.at[2], mup.at[1], down_y),
            (hw.at[1], hup.at[0], down_x), (hw.at[2], hup.at[1], down_y),
        )[k]
        return remote(src, dst, wsend.at[k], wrecv.at[k], peer)

    above = []
    for k in range(4):
        guarded((low_x, low_y)[k % 2], lambda: weights(k).start())
        Once(lambda k=k: guarded((low_x, low_y)[k % 2], lambda: weights(k).wait_send()), finish)
        above.append(
            Once(lambda k=k: guarded((high_x, high_y)[k % 2], lambda: weights(k).wait_recv()), finish)
        )
    col[...] = jnp.zeros_like(col)
    msc[...] = jnp.zeros_like(msc)

    get_z.wait()
    inner = times(q0[...], zf[...]).astype(BF16)
    w0[...] = times_t(inner, zf[...])
    get_c.wait()
    uv[:, :256] = times(q0[...], cf[...])
    get_h.wait()
    hb[...] = h0[...].astype(BF16)
    get_b.wait()
    bh[...] = times_t(times(hb[...], bf[...]).astype(BF16), bf[...])
    for copy in above:
        copy.wait()

    def near(total, w, up, values, nb, rows, cols=slice(None)):
        diag, wx, wy, wp = w[0], w[1], w[2], w[3]
        ux, uy = up[0], up[1]
        total = total + (diag + wx + ux + wy + uy + wp) * values
        total = total - wx * nb[0, rows, cols].astype(F32) - ux * nb[1, rows, cols].astype(F32)
        return total - wy * nb[2, rows, cols].astype(F32) - uy * nb[3, rows, cols].astype(F32)

    q_arrive()

    def body(rows):
        w0[rows, :] = near(w0[rows, :], mw, mup, q0[rows, :].astype(F32), qn, rows)

    row_loop(body)
    q_sent((4,))
    h_start()
    q_arrive((4,))

    def body(rows):
        w = w0[rows, :] - mw[3] * qn[4, rows, :].astype(F32)
        w0[rows, :] = w
        wb[rows, :] = w.astype(BF16)

    row_loop(body)
    w_start()
    uv[:, 256:] = times(wb[...], cf[...])
    uvb[...] = uv[...].astype(BF16)

    def moments(r, w, b, inner, weight):
        def body(rows):
            rv, wv, bv = r[rows, :], w[rows, :], b[rows, :].astype(F32)
            col[rows, 0:1] = lanes(rv * rv)
            col[rows, 1:2] = lanes(rv * wv)
            col[rows, 2:3] = lanes(wv * wv)
            col[rows, 3:4] = lanes(bv * wv)
            col[rows, 4:5] = lanes(weight[0] * bv * bv) + lanes(inner[rows, :] * inner[rows, :])

        row_loop(body)

    def edges(b, nb, weight, up):
        ends = jnp.where(low_x, 0.0, weight[1]) + jnp.where(low_y, 0.0, weight[2])

        def body(rows):
            bv = b[rows, :].astype(F32)
            dx, dy = bv - nb[0, rows, :].astype(F32), bv - nb[2, rows, :].astype(F32)
            col[rows, 4:5] += lanes(weight[1] * dx * dx + weight[2] * dy * dy)

        row_loop(body, HALF)

        def body(n, carry):
            rows = pl.ds(pl.multiple_of(n * ROWS, ROWS), ROWS)
            upper = pl.ds(pl.multiple_of(HALF + n * ROWS, ROWS), ROWS)
            bv = b[upper, :].astype(F32)
            dx, dy = bv - nb[1, rows, :].astype(F32), bv - nb[3, rows, :].astype(F32)
            col[upper, 4:5] += lanes(up[0] * dx * dx + up[1] * dy * dy + ends * bv * bv)
            return carry

        lax.fori_loop(0, HALF // ROWS, body, 0)

    def face_edges(b, there, weight):
        def body(n, carry):
            rows = pl.ds(pl.multiple_of(n * ROWS, ROWS), ROWS)
            own = pl.ds(pl.multiple_of(f * HALF + n * ROWS, ROWS), ROWS)
            d = b[own, :].astype(F32) - there(rows, own).astype(F32)
            col[own, 4:5] += lanes(weight[3] * d * d)
            return carry

        lax.fori_loop(0, HALF // ROWS, body, 0)

    def sum_start(buf, slot, peers, k):
        for peer in peers:
            remote(mom.at[k], buf.at[slot], asend.at[k], arecv.at[k], peer).start()
        buf[slot] = mom[k]
        rest = buf.at[pl.ds(0, buf.shape[0] - 1)]
        arrived = Once(lambda: pltpu.make_async_copy(rest, rest, arecv.at[k]).wait(), finish)
        Once(lambda: pltpu.make_async_copy(rest, rest, asend.at[k]).wait(), finish)

        def end():
            arrived.wait()
            return jnp.sum(buf[...], axis=0)

        return end

    xm[...] = times(wb[...], zf[...])
    moments(r0, w0, wb, xm, mw)
    w_sent((4,))
    uv_start()
    w_arrive()
    edges(wb, wn, mw, mup)
    w_arrive((4,))
    face_edges(wb, lambda rows, own: wn[4, rows, :], mw)
    mom[0] = jnp.transpose(col[...])[:8, :]
    sum_arx1 = sum_start(arx1, x_slot, x_peers, 0)

    for k in range(2):
        cols = slice(256 * k, 256 * k + 256)
        buv[:, cols] = times_t(times(uvb[:, cols], bf[...]).astype(BF16), bf[...])
    h_arrive((0, 1, 2, 3, 4))

    def body(rows):
        total = near(bh[rows, :], hw, hup, hb[rows, :].astype(F32), hn, rows)
        bh[rows, :] = total - hw[3] * hn[4, rows, :].astype(F32)

    row_loop(body)
    mom[1] = sum_arx1()
    sum_ary1 = sum_start(ary1, y_slot, y_peers, 1)
    uv_arrive((0, 1, 2, 3, 4))

    def body(rows):
        for k in range(2):
            cols = slice(256 * k, 256 * k + 256)
            total = near(buv[rows, cols], hw, hup, uvb[rows, cols].astype(F32), uvn, rows, cols)
            buv[rows, cols] = total - hw[3] * uvn[4, rows, cols].astype(F32)

    row_loop(body)

    def columns(pair):
        msc[0:1, :] = pair[0]
        msc[1:2, :] = pair[1]
        col[...] = jnp.transpose(msc[...])

    total = sum_ary1()
    columns(step_sizes(total))

    def body(rows):
        a, b = col[rows, 0:1], col[rows, 1:2]
        image = bh[rows, :] - a * buv[rows, :256] - b * buv[rows, 256:]
        bs[rows, :] = image
        bsb[rows, :] = image.astype(BF16)

    row_loop(body)
    b_start()
    get_b2 = face_send(0, bsb.at[mine], bsp.at[mine])
    for copy in get_sh:
        copy.wait()
    get_shp = face_send(1, sh.at[1 - f], shp)

    def body(n, energy):
        rows = pl.ds(pl.multiple_of(n * ROWS, ROWS), ROWS)
        a, b = col[rows, 0:1], col[rows, 1:2]
        s0[rows, :] = h0[rows, :] - a * uv[rows, :256] - b * uv[rows, 256:]
        sp[rows, :] = (
            hn[4, rows, :].astype(F32)
            - a * uvn[4, rows, :256].astype(F32)
            - b * uvn[4, rows, 256:].astype(F32)
        )
        x = a * r0[rows, :] + b * w0[rows, :]
        out_m[0, 0, 0, rows, :] = x
        return energy + jnp.sum(x * x, axis=0, keepdims=True)

    energy = lax.fori_loop(0, LOADS // ROWS, body, jnp.zeros((1, r0.shape[1]), F32))
    get_sm.wait()
    sens = times(jnp.broadcast_to(energy.astype(BF16), (16, energy.shape[1])), sm[...])
    part[0] = sens[:8, :128]
    part[1] = sens[:8, 128:]
    get_part = face_send(2, part.at[1 - f], got)
    xh[...] = times(bsb[...], bf[...])
    moments(s0, bs, bsb, xh, hw)
    b_arrive()
    edges(bsb, bsn, hw, hup)
    b_arrive((4,))
    face_edges(bsb, lambda rows, own: bsp[own, :], hw)
    mom[2] = jnp.transpose(col[...])[:8, :]
    sum_arx2 = sum_start(arx2, x_slot, x_peers, 2)
    for copy in get_last:
        copy.wait()
    kinds = mat[...]
    stiffness = jnp.zeros(kinds.shape, F32)
    for k in range(scale.shape[0]):
        stiffness = jnp.where(kinds == k, scale[k], stiffness)
    factor = -3.0 * den[...] * den[...] * stiffness / LOADS
    get_b2.wait()
    get_part.wait()
    get_shp.wait()
    sens = part[f, 0:1, :] + got[0:1, :]
    mom[3] = sum_arx2()
    sum_ary2 = sum_start(ary2, y_slot, y_peers, 3)
    total = sum_ary2()
    columns(step_sizes(total))

    def body(n, energies):
        rows = pl.ds(pl.multiple_of(n * ROWS, ROWS), ROWS)
        a, b = col[rows, 0:1], col[rows, 1:2]
        x = a * s0[rows, :] + b * bs[rows, :]
        out_h[0, 0, 0, rows, :] = x
        there = a * sp[rows, :] + b * bsp[rows, :].astype(F32)
        return (
            energies[0] + jnp.sum(x * x, axis=0, keepdims=True),
            energies[1] + jnp.sum(there * there, axis=0, keepdims=True),
        )

    zero = jnp.zeros((1, h0.shape[1]), F32)
    energies = lax.fori_loop(0, LOADS // ROWS, body, (zero, zero))
    for energy, table in zip(energies, (sh[f], shp[...])):
        wide = jnp.broadcast_to(energy.astype(BF16), (16, energy.shape[1]))
        sens = sens + times(wide, table)[0:1, :]
    out_g[0] = factor * sens
    close()


def place(a, b, c, x, y, z, sem):
    copies = [
        pltpu.make_async_copy(src, dst, sem.at[k])
        for k, (src, dst) in enumerate(((a, x), (b, y), (c, z)))
    ]
    for copy in copies:
        copy.start()
    for copy in copies:
        copy.wait()


def solution(mesh):
    nx, ny = mesh.shape["gx"], mesh.shape["gy"]
    zs = 8 if nx % 8 == 0 else 1
    xs = nx // zs

    def vm(*shape, dtype=F32):
        return pltpu.VMEM(shape, dtype)

    def bm(*shape):
        return pltpu.VMEM(shape, BF16)

    in_hbm = pl.BlockSpec(memory_space=pltpu.HBM)
    in_vmem = pl.BlockSpec(memory_space=pltpu.VMEM)
    sems = pltpu.SemaphoreType.DMA
    outs = (
        jax.ShapeDtypeStruct((1, 1, 1, 128, 768), F32),
        jax.ShapeDtypeStruct((1, 1, 1, 128, 256), F32),
        jax.ShapeDtypeStruct((1, 1, 128), F32),
    )

    def on_device(*args):
        results = pl.pallas_call(
            functools.partial(kernel, nx, ny, xs, zs),
            out_shape=outs,
            in_specs=[in_hbm] * 18,
            out_specs=(in_vmem,) * 3,
            scratch_shapes=[
                vm(128, 768), vm(128, 256), bm(768, 768), bm(256, 256),
                vm(4, 1, 768), vm(4, 1, 256), vm(2, 1, 768), vm(2, 1, 256),
                bm(768, 256), bm(768, 256), bm(2, 256, 128), bm(256, 128),
                vm(1, 128), vm(1, 128, dtype=jnp.int32), pltpu.SMEM((8,), F32),
                bm(128, 768), bm(5, 128, 768), vm(128, 768), bm(128, 768), bm(5, 64, 768),
                bm(128, 256), bm(5, 128, 256), vm(128, 256),
                vm(128, 512), bm(128, 512), bm(5, 128, 512), vm(128, 512),
                vm(128, 256), vm(128, 256), vm(128, 256), bm(128, 256), bm(4, 64, 256),
                bm(128, 256),
                vm(128, 128), vm(128, 128), vm(4, 8, 128),
                vm(nx, 8, 128), vm(ny * 2, 8, 128), vm(nx, 8, 128), vm(ny * 2, 8, 128),
                vm(128, 768), vm(128, 256), vm(2, 8, 128), vm(8, 128),
                sems((64,)), sems((4,)), sems((4,)), sems((25,)), sems((25,)),
                sems((4,)), sems((4,)), sems((3,)), sems((3,)),
            ],
            compiler_params=pltpu.CompilerParams(
                collective_id=0, has_side_effects=True, vmem_limit_bytes=32 * 1024 * 1024
            ),
        )(*(pltpu.with_memory_space_constraint(a, pltpu.HBM) for a in args))
        return pl.pallas_call(
            place,
            out_shape=outs,
            in_specs=[in_vmem] * 3,
            out_specs=[in_hbm] * 3,
            scratch_shapes=[sems((3,))],
        )(*(pltpu.with_memory_space_constraint(a, pltpu.VMEM) for a in results))

    block = P("gx", "gy", "phys", None, None)
    line = P("gx", "gy", "phys", None)
    both = P("gx", "gy", None)
    part = P("gx", "gy", "phys")
    return jax.shard_map(
        on_device,
        mesh=mesh,
        in_specs=(
            block, block, block, block, line, line, line, line, both, line, line, both,
            block, block, block, part, part, P(),
        ),
        out_specs=(block, block, part),
        check_vma=False,
    )
```

time: 97.8 us -> 76.1 us (0.78)
  local copies, waits for them, and re-layouts: 16.3 us -> 0 us
  Pallas kernels: 80.3 us -> 75.3 us
    unnamed x39 -> x0, local copies, waits for them, and re-layouts: 16.3 us -> none
    pallas_call x1 -> x2, Pallas kernels: 80.3 us -> 75.3 us  [the longest x1 74.5 us: on_device(): pl.pallas_call(functools.partial(kernel, nx, ny, xs, zs), out_shape=outs,...]
where the time goes in v2:
time: 76.1 us; the launch traced here: 75.9 us
  Pallas kernels  75.3 us (99%)
    pallas_call x1, Pallas kernels, on_device(): pl.pallas_call(functools.partial(kernel, nx, ny, xs, zs), out_shape=outs,...  74.5 us

profile of v2, /device:TPU:1, one launch (start us, length us, event | category | flops | bytes accessed | tf_op | source)
XLA Modules:
  0.0 75.9 jit_solution(13327589123010930951)
XLA Ops:
  0.6 74.5 %shard_map.193 = (f32[1,1,1,128,768]{4,3,2,1,0:T(8,128)S(1)}, f32[1,1,1,128,256]{4,3,2,1,0:T(8,128)S(1)}, f32[1,1,128]{2,1,0:T(1,128)S(1)}) custom-call(f32[1,1,1,128,768]{4,3,2,1,0:T(8,128)} %ml.1, f32[1,1,1,128,256]{4,3,2,1,0:T(8,128)} %hl.1, bf16[1,1,1,768,768]{4,3,2,1,0:T(8,128)(2,1)} %mf.1, bf16[1,1,1,256,256]{4,3,2,1,0:T(8,128)(2,1)} %hf.1, ...), custom_call_target="tpu_custom_call" | custom-call | tf_op jit(solution)/shard_map/pallas_call | solution.py:456
  75.1 0.8 %shard_map.194 = (f32[1,1,1,128,768]{4,3,2,1,0:T(8,128)}, f32[1,1,1,128,256]{4,3,2,1,0:T(8,128)}, f32[1,1,128]{2,1,0:T(1,128)}) custom-call(f32[1,1,1,128,768]{4,3,2,1,0:T(8,128)S(1)} %get-tuple-element.6.a, f32[1,1,1,128,256]{4,3,2,1,0:T(8,128)S(1)} %get-tuple-element.7.b, f32[1,1,128]{2,1,0:T(1,128)S(1)} %get-tuple-element.8.c), custom_call_target="tpu_custom_call" | custom-call | tf_op jit(solution)/shard_map/pallas_call | solution.py:481

commit v3 on v2

--- a/solution.py
+++ b/solution.py
@@ -13,6 +13,7 @@
 ROWS = 16
 LOADS = 128
 HALF = LOADS // 2
+QUARTER = LOADS // 4
 
 
 def ring(k, n):
@@ -36,16 +37,23 @@
             self.pending = None
 
 
-def row_loop(body, count=LOADS):
+def row_loop(body, count=LOADS, first=0):
     def step(n, carry):
-        body(pl.ds(pl.multiple_of(n * ROWS, ROWS), ROWS))
+        body(pl.ds(pl.multiple_of(first + n * ROWS, ROWS), ROWS))
         return carry
 
     lax.fori_loop(0, count // ROWS, step, 0)
 
 
-def lanes(x):
-    return jnp.sum(x, axis=1, keepdims=True)
+def fold(x):
+    return sum(x[:, k : k + 128] for k in range(0, x.shape[1], 128))
+
+
+def lane_sums(parts):
+    return lax.dot_general(
+        jnp.ones((8, 128), F32), parts, (((1,), (1,)), ((), ())),
+        precision=lax.Precision.HIGHEST, preferred_element_type=F32,
+    )
 
 
 def times(a, b):
@@ -72,7 +80,7 @@
     out_m, out_h, out_g,
     r0, h0, zf, bf, mw, hw, mup, hup, cf, sm, sh, shp, den, mat, scale,
     q0, qn, w0, wb, wn, hb, hn, bh, uv, uvb, uvn, buv, s0, sp, bs, bsb, bsn, bsp,
-    msc, col, mom, arx1, ary1, arx2, ary2, xm, xh, part, got,
+    msc, col, pm, mom, arx1, ary1, arx2, ary2, xm, xh, part, got,
     lsem, wsend, wrecv, esend, erecv, asend, arecv, fsend, frecv,
 ):
     i, j, f = lax.axis_index("gx"), lax.axis_index("gy"), lax.axis_index("phys")
@@ -116,7 +124,7 @@
         for piece in finish:
             piece.wait()
 
-    get_r0 = load(ml.at[0, 0, 0], r0)
+    get_r0 = [load(ml.at[0, 0, 0, pl.ds(HALF * c, HALF)], r0.at[pl.ds(HALF * c, HALF)]) for c in range(2)]
     barrier = pltpu.get_barrier_semaphore()
     for peer in y_peers + x_peers:
         pl.semaphore_signal(barrier, inc=1, device_id=peer, device_id_type=MESH)
@@ -126,6 +134,7 @@
         def _():
             for ref in (qn, wn, hn, uvn, bsn):
                 ref[d] = jnp.zeros_like(ref[d])
+            uvn[5 + d] = jnp.zeros_like(uvn[d])
     for d, there in ((0, high_x), (1, high_y)):
         @pl.when(jnp.logical_not(there))
         def _():
@@ -159,10 +168,27 @@
     mine = pl.ds(pl.multiple_of(f * HALF, HALF), HALF)
     yours = pl.ds(pl.multiple_of((1 - f) * HALF, HALF), HALF)
     half = (low, high, low, high, yours)
-    q_start, q_arrive, q_sent = exchange(0, lambda d: q0, lambda d: qn.at[d])
+    chunks = [pl.ds(HALF * c, HALF) for c in range(2)]
+    q_sends = [
+        exchange(s, lambda d, c=c: q0.at[chunks[c]], lambda d, c=c: qn.at[d, chunks[c]])
+        for c, s in enumerate((0, 6))
+    ]
+
+    def ends_of(d, c):
+        shift = (0, QUARTER, 0, QUARTER, (1 - f) * QUARTER)[d]
+        return pl.ds(pl.multiple_of(HALF * c + shift, QUARTER), QUARTER)
+
+    w_sends = [
+        exchange(
+            s,
+            lambda d, c=c: wb.at[ends_of(d, c)],
+            lambda d, c=c: wn.at[d, pl.ds(QUARTER * c, QUARTER)],
+        )
+        for c, s in enumerate((2, 7))
+    ]
     h_start, h_arrive, h_sent = exchange(1, lambda d: hb, lambda d: hn.at[d])
-    w_start, w_arrive, w_sent = exchange(2, lambda d: wb.at[half[d]], lambda d: wn.at[d])
-    uv_start, uv_arrive, uv_sent = exchange(3, lambda d: uvb, lambda d: uvn.at[d])
+    u_start, u_arrive, u_sent = exchange(3, lambda d: uvb.at[0], lambda d: uvn.at[d])
+    v_start, v_arrive, v_sent = exchange(5, lambda d: uvb.at[1], lambda d: uvn.at[5 + d])
     b_start, b_arrive, b_sent = exchange(
         4, lambda d: bsb.at[half[d]], lambda d: bsp.at[yours] if d == 4 else bsn.at[d]
     )
@@ -173,10 +199,12 @@
         Once(copy.wait_send, finish)
         return Once(copy.wait_recv, finish)
 
-    get_r0.wait()
-    q0[...] = r0[...].astype(BF16)
-    pl.semaphore_wait(barrier, len(x_peers) + len(y_peers))
-    q_start()
+    for c, (start, _, _) in enumerate(q_sends):
+        get_r0[c].wait()
+        q0[chunks[c], :] = r0[chunks[c], :].astype(BF16)
+        if c == 0:
+            pl.semaphore_wait(barrier, len(x_peers) + len(y_peers))
+        start()
     small = [
         load(md.at[0, 0], mw.at[0]), load(mx.at[0, 0], mw.at[1]), load(my.at[0, 0], mw.at[2]),
         load(mp.at[0], mw.at[3]),
@@ -207,7 +235,7 @@
         above.append(
             Once(lambda k=k: guarded((high_x, high_y)[k % 2], lambda: weights(k).wait_recv()), finish)
         )
-    col[...] = jnp.zeros_like(col)
+    mom[...] = jnp.zeros_like(mom)
     msc[...] = jnp.zeros_like(msc)
 
     get_z.wait()
@@ -215,6 +243,7 @@
     w0[...] = times_t(inner, zf[...])
     get_c.wait()
     uv[:, :256] = times(q0[...], cf[...])
+    uvb[0] = uv[:, :256].astype(BF16)
     get_h.wait()
     hb[...] = h0[...].astype(BF16)
     get_b.wait()
@@ -229,66 +258,77 @@
         total = total - wx * nb[0, rows, cols].astype(F32) - ux * nb[1, rows, cols].astype(F32)
         return total - wy * nb[2, rows, cols].astype(F32) - uy * nb[3, rows, cols].astype(F32)
 
-    q_arrive()
-
-    def body(rows):
-        w0[rows, :] = near(w0[rows, :], mw, mup, q0[rows, :].astype(F32), qn, rows)
-
-    row_loop(body)
-    q_sent((4,))
-    h_start()
-    q_arrive((4,))
-
-    def body(rows):
-        w = w0[rows, :] - mw[3] * qn[4, rows, :].astype(F32)
-        w0[rows, :] = w
-        wb[rows, :] = w.astype(BF16)
-
-    row_loop(body)
-    w_start()
+    for c in range(2):
+        start, arrive, sent = q_sends[c]
+        arrive()
+
+        def body(rows):
+            w0[rows, :] = near(w0[rows, :], mw, mup, q0[rows, :].astype(F32), qn, rows)
+
+        row_loop(body, HALF, HALF * c)
+        arrive((4,))
+
+        def body(rows):
+            w = w0[rows, :] - mw[3] * qn[4, rows, :].astype(F32)
+            w0[rows, :] = w
+            wb[rows, :] = w.astype(BF16)
+
+        row_loop(body, HALF, HALF * c)
+        if c == 0:
+            q_sends[1][2]((4,))
+        else:
+            w_sends[0][2]((4,))
+        w_sends[c][0]()
+    u_start((0, 1))
+    h_start((0, 1))
     uv[:, 256:] = times(wb[...], cf[...])
-    uvb[...] = uv[...].astype(BF16)
-
-    def moments(r, w, b, inner, weight):
+    uvb[1] = uv[:, 256:].astype(BF16)
+    v_start((0, 1))
+
+    def moments(k, r, w, b, inner, weight):
         def body(rows):
             rv, wv, bv = r[rows, :], w[rows, :], b[rows, :].astype(F32)
-            col[rows, 0:1] = lanes(rv * rv)
-            col[rows, 1:2] = lanes(rv * wv)
-            col[rows, 2:3] = lanes(wv * wv)
-            col[rows, 3:4] = lanes(bv * wv)
-            col[rows, 4:5] = lanes(weight[0] * bv * bv) + lanes(inner[rows, :] * inner[rows, :])
+            iv = inner[rows, :]
+            pm[0, rows, :] = fold(rv * rv)
+            pm[1, rows, :] = fold(rv * wv)
+            pm[2, rows, :] = fold(wv * wv)
+            pm[3, rows, :] = fold(bv * wv)
+            pm[4, rows, :] = fold(weight[0] * bv * bv + iv * iv)
 
         row_loop(body)
-
-    def edges(b, nb, weight, up):
+        sums = lane_sums(pm[:4].reshape(4 * LOADS, 128))
+        for n in range(4):
+            mom[k, n : n + 1, :] = sums[0:1, n * LOADS : (n + 1) * LOADS]
+
+    def moments_end(k):
+        mom[k, 4:5, :] = lane_sums(pm[4])[0:1, :]
+
+    def edges(b, nb, weight, up, first, there, count):
         ends = jnp.where(low_x, 0.0, weight[1]) + jnp.where(low_y, 0.0, weight[2])
 
-        def body(rows):
-            bv = b[rows, :].astype(F32)
+        def body(n, carry):
+            rows = pl.ds(pl.multiple_of(there + n * ROWS, ROWS), ROWS)
+            lower = pl.ds(pl.multiple_of(first + n * ROWS, ROWS), ROWS)
+            bv = b[lower, :].astype(F32)
             dx, dy = bv - nb[0, rows, :].astype(F32), bv - nb[2, rows, :].astype(F32)
-            col[rows, 4:5] += lanes(weight[1] * dx * dx + weight[2] * dy * dy)
-
-        row_loop(body, HALF)
-
-        def body(n, carry):
-            rows = pl.ds(pl.multiple_of(n * ROWS, ROWS), ROWS)
-            upper = pl.ds(pl.multiple_of(HALF + n * ROWS, ROWS), ROWS)
+            pm[4, lower, :] += fold(weight[1] * dx * dx + weight[2] * dy * dy)
+            upper = pl.ds(pl.multiple_of(first + count + n * ROWS, ROWS), ROWS)
             bv = b[upper, :].astype(F32)
             dx, dy = bv - nb[1, rows, :].astype(F32), bv - nb[3, rows, :].astype(F32)
-            col[upper, 4:5] += lanes(up[0] * dx * dx + up[1] * dy * dy + ends * bv * bv)
+            pm[4, upper, :] += fold(up[0] * dx * dx + up[1] * dy * dy + ends * bv * bv)
             return carry
 
-        lax.fori_loop(0, HALF // ROWS, body, 0)
-
-    def face_edges(b, there, weight):
+        lax.fori_loop(0, count // ROWS, body, 0)
+
+    def face_edges(b, other_face, weight, first, there, count):
         def body(n, carry):
-            rows = pl.ds(pl.multiple_of(n * ROWS, ROWS), ROWS)
-            own = pl.ds(pl.multiple_of(f * HALF + n * ROWS, ROWS), ROWS)
-            d = b[own, :].astype(F32) - there(rows, own).astype(F32)
-            col[own, 4:5] += lanes(weight[3] * d * d)
+            rows = pl.ds(pl.multiple_of(there + n * ROWS, ROWS), ROWS)
+            own = pl.ds(pl.multiple_of(first + f * count + n * ROWS, ROWS), ROWS)
+            d = b[own, :].astype(F32) - other_face(rows, own).astype(F32)
+            pm[4, own, :] += fold(weight[3] * d * d)
             return carry
 
-        lax.fori_loop(0, HALF // ROWS, body, 0)
+        lax.fori_loop(0, count // ROWS, body, 0)
 
     def sum_start(buf, slot, peers, k):
         for peer in peers:
@@ -305,19 +345,22 @@
         return end
 
     xm[...] = times(wb[...], zf[...])
-    moments(r0, w0, wb, xm, mw)
-    w_sent((4,))
-    uv_start()
-    w_arrive()
-    edges(wb, wn, mw, mup)
-    w_arrive((4,))
-    face_edges(wb, lambda rows, own: wn[4, rows, :], mw)
-    mom[0] = jnp.transpose(col[...])[:8, :]
+    moments(0, r0, w0, wb, xm, mw)
+    w_sends[1][2]((4,))
+    h_start((4, 2, 3))
+    u_start((4, 2, 3))
+    for c in range(2):
+        w_sends[c][1]()
+        edges(wb, wn, mw, mup, HALF * c, QUARTER * c, QUARTER)
+        w_sends[c][1]((4,))
+        face_edges(wb, lambda rows, own: wn[4, rows, :], mw, HALF * c, QUARTER * c, QUARTER)
+    moments_end(0)
     sum_arx1 = sum_start(arx1, x_slot, x_peers, 0)
+    v_start((4, 2, 3))
 
     for k in range(2):
         cols = slice(256 * k, 256 * k + 256)
-        buv[:, cols] = times_t(times(uvb[:, cols], bf[...]).astype(BF16), bf[...])
+        buv[:, cols] = times_t(times(uvb[k], bf[...]).astype(BF16), bf[...])
     h_arrive((0, 1, 2, 3, 4))
 
     def body(rows):
@@ -327,13 +370,15 @@
     row_loop(body)
     mom[1] = sum_arx1()
     sum_ary1 = sum_start(ary1, y_slot, y_peers, 1)
-    uv_arrive((0, 1, 2, 3, 4))
+    u_arrive((0, 1, 2, 3, 4))
+    v_arrive((0, 1, 2, 3, 4))
 
     def body(rows):
         for k in range(2):
             cols = slice(256 * k, 256 * k + 256)
-            total = near(buv[rows, cols], hw, hup, uvb[rows, cols].astype(F32), uvn, rows, cols)
-            buv[rows, cols] = total - hw[3] * uvn[4, rows, cols].astype(F32)
+            there = uvn.at[5 * k : 5 * k + 5]
+            total = near(buv[rows, cols], hw, hup, uvb[k, rows, :].astype(F32), there, rows)
+            buv[rows, cols] = total - hw[3] * there[4, rows, :].astype(F32)
 
     row_loop(body)
 
@@ -353,10 +398,6 @@
 
     row_loop(body)
     b_start()
-    get_b2 = face_send(0, bsb.at[mine], bsp.at[mine])
-    for copy in get_sh:
-        copy.wait()
-    get_shp = face_send(1, sh.at[1 - f], shp)
 
     def body(n, energy):
         rows = pl.ds(pl.multiple_of(n * ROWS, ROWS), ROWS)
@@ -364,8 +405,8 @@
         s0[rows, :] = h0[rows, :] - a * uv[rows, :256] - b * uv[rows, 256:]
         sp[rows, :] = (
             hn[4, rows, :].astype(F32)
-            - a * uvn[4, rows, :256].astype(F32)
-            - b * uvn[4, rows, 256:].astype(F32)
+            - a * uvn[4, rows, :].astype(F32)
+            - b * uvn[9, rows, :].astype(F32)
         )
         x = a * r0[rows, :] + b * w0[rows, :]
         out_m[0, 0, 0, rows, :] = x
@@ -376,15 +417,19 @@
     sens = times(jnp.broadcast_to(energy.astype(BF16), (16, energy.shape[1])), sm[...])
     part[0] = sens[:8, :128]
     part[1] = sens[:8, 128:]
+    xh[...] = times(bsb[...], bf[...])
+    moments(2, s0, bs, bsb, xh, hw)
+    b_arrive()
+    edges(bsb, bsn, hw, hup, 0, 0, HALF)
+    b_arrive((4,))
+    face_edges(bsb, lambda rows, own: bsp[own, :], hw, 0, 0, HALF)
+    moments_end(2)
+    sum_arx2 = sum_start(arx2, x_slot, x_peers, 2)
+    get_b2 = face_send(0, bsb.at[mine], bsp.at[mine])
     get_part = face_send(2, part.at[1 - f], got)
-    xh[...] = times(bsb[...], bf[...])
-    moments(s0, bs, bsb, xh, hw)
-    b_arrive()
-    edges(bsb, bsn, hw, hup)
-    b_arrive((4,))
-    face_edges(bsb, lambda rows, own: bsp[own, :], hw)
-    mom[2] = jnp.transpose(col[...])[:8, :]
-    sum_arx2 = sum_start(arx2, x_slot, x_peers, 2)
+    for copy in get_sh:
+        copy.wait()
+    get_shp = face_send(1, sh.at[1 - f], shp)
     for copy in get_last:
         copy.wait()
     kinds = mat[...]
@@ -392,12 +437,12 @@
     for k in range(scale.shape[0]):
         stiffness = jnp.where(kinds == k, scale[k], stiffness)
     factor = -3.0 * den[...] * den[...] * stiffness / LOADS
+    mom[3] = sum_arx2()
+    sum_ary2 = sum_start(ary2, y_slot, y_peers, 3)
     get_b2.wait()
     get_part.wait()
     get_shp.wait()
     sens = part[f, 0:1, :] + got[0:1, :]
-    mom[3] = sum_arx2()
-    sum_ary2 = sum_start(ary2, y_slot, y_peers, 3)
     total = sum_ary2()
     columns(step_sizes(total))
 
@@ -465,13 +510,13 @@
                 vm(1, 128), vm(1, 128, dtype=jnp.int32), pltpu.SMEM((8,), F32),
                 bm(128, 768), bm(5, 128, 768), vm(128, 768), bm(128, 768), bm(5, 64, 768),
                 bm(128, 256), bm(5, 128, 256), vm(128, 256),
-                vm(128, 512), bm(128, 512), bm(5, 128, 512), vm(128, 512),
+                vm(128, 512), bm(2, 128, 256), bm(10, 128, 256), vm(128, 512),
                 vm(128, 256), vm(128, 256), vm(128, 256), bm(128, 256), bm(4, 64, 256),
                 bm(128, 256),
-                vm(128, 128), vm(128, 128), vm(4, 8, 128),
+                vm(128, 128), vm(128, 128), vm(5, 128, 128), vm(4, 8, 128),
                 vm(nx, 8, 128), vm(ny * 2, 8, 128), vm(nx, 8, 128), vm(ny * 2, 8, 128),
                 vm(128, 768), vm(128, 256), vm(2, 8, 128), vm(8, 128),
-                sems((64,)), sems((4,)), sems((4,)), sems((25,)), sems((25,)),
+                sems((64,)), sems((4,)), sems((4,)), sems((40,)), sems((40,)),
                 sems((4,)), sems((4,)), sems((3,)), sems((3,)),
             ],
             compiler_params=pltpu.CompilerParams(

time: 76.1 us -> 70.8 us (0.930)
  Pallas kernels: 75.3 us -> 70 us
    pallas_call x1, Pallas kernels: 74.5 us -> 69.2 us  [on_device(): pl.pallas_call(functools.partial(kernel, nx, ny, xs, zs), out_shape=outs,...]
where the time goes in v3:
time: 70.8 us; the launch traced here: 70.7 us
  Pallas kernels  70 us (99%)
    pallas_call x1, Pallas kernels, on_device(): pl.pallas_call(functools.partial(kernel, nx, ny, xs, zs), out_shape=outs,...  69.2 us

profile of v3, /device:TPU:1, one launch (start us, length us, event | category | flops | bytes accessed | tf_op | source)
XLA Modules:
  0.0 70.7 jit_solution(7105682152161817361)
XLA Ops:
  0.6 69.2 %shard_map.193 = (f32[1,1,1,128,768]{4,3,2,1,0:T(8,128)S(1)}, f32[1,1,1,128,256]{4,3,2,1,0:T(8,128)S(1)}, f32[1,1,128]{2,1,0:T(1,128)S(1)}) custom-call(f32[1,1,1,128,768]{4,3,2,1,0:T(8,128)} %ml.1, f32[1,1,1,128,256]{4,3,2,1,0:T(8,128)} %hl.1, bf16[1,1,1,768,768]{4,3,2,1,0:T(8,128)(2,1)} %mf.1, bf16[1,1,1,256,256]{4,3,2,1,0:T(8,128)(2,1)} %hf.1, ...), custom_call_target="tpu_custom_call" | custom-call | tf_op jit(solution)/shard_map/pallas_call | solution.py:501
  69.8 0.8 %shard_map.194 = (f32[1,1,1,128,768]{4,3,2,1,0:T(8,128)}, f32[1,1,1,128,256]{4,3,2,1,0:T(8,128)}, f32[1,1,128]{2,1,0:T(1,128)}) custom-call(f32[1,1,1,128,768]{4,3,2,1,0:T(8,128)S(1)} %get-tuple-element.6.a, f32[1,1,1,128,256]{4,3,2,1,0:T(8,128)S(1)} %get-tuple-element.7.b, f32[1,1,128]{2,1,0:T(1,128)S(1)} %get-tuple-element.8.c), custom_call_target="tpu_custom_call" | custom-call | tf_op jit(solution)/shard_map/pallas_call | solution.py:526

commit v4 on v3

--- a/solution.py
+++ b/solution.py
@@ -13,7 +13,9 @@
 ROWS = 16
 LOADS = 128
 HALF = LOADS // 2
-QUARTER = LOADS // 4
+PIECES = 4
+PIECE = LOADS // PIECES
+END = PIECE // 2
 
 
 def ring(k, n):
@@ -124,11 +126,75 @@
         for piece in finish:
             piece.wait()
 
-    get_r0 = [load(ml.at[0, 0, 0, pl.ds(HALF * c, HALF)], r0.at[pl.ds(HALF * c, HALF)]) for c in range(2)]
+    pieces = [pl.ds(PIECE * c, PIECE) for c in range(PIECES)]
+    get_r0 = [load(ml.at[0, 0, 0, piece], r0.at[piece]) for piece in pieces]
     barrier = pltpu.get_barrier_semaphore()
     for peer in y_peers + x_peers:
         pl.semaphore_signal(barrier, inc=1, device_id=peer, device_id_type=MESH)
 
+    def exchange(stage, src_of, dst_of):
+        receipts, departures = {}, {}
+
+        def copy(d):
+            k = stage * 5 + d
+            return remote(src_of(d), dst_of(d), esend.at[k], erecv.at[k], target[d])
+
+        def start(order=(4, 0, 1, 2, 3)):
+            for d in order:
+                guarded(sends[d], lambda: copy(d).start())
+                receipts[d] = Once(lambda d=d: guarded(gets[d], copy(d).wait_recv), finish)
+                departures[d] = Once(lambda d=d: guarded(sends[d], copy(d).wait_send), finish)
+
+        def arrive(order=(0, 1, 2, 3)):
+            for d in order:
+                receipts[d].wait()
+
+        def sent(order):
+            for d in order:
+                departures[d].wait()
+
+        return start, arrive, sent
+
+    low, high = pl.ds(0, HALF), pl.ds(HALF, HALF)
+    mine = pl.ds(pl.multiple_of(f * HALF, HALF), HALF)
+    yours = pl.ds(pl.multiple_of((1 - f) * HALF, HALF), HALF)
+    half = (low, high, low, high, yours)
+    q_sends = [
+        exchange(s, lambda d, c=c: q0.at[pieces[c]], lambda d, c=c: qn.at[d, pieces[c]])
+        for c, s in enumerate((0, 6, 8, 9)[:PIECES])
+    ]
+
+    def ends_of(d, c):
+        shift = (0, END, 0, END, (1 - f) * END)[d]
+        return pl.ds(pl.multiple_of(PIECE * c + shift, END), END)
+
+    w_sends = [
+        exchange(
+            s,
+            lambda d, c=c: wb.at[ends_of(d, c)],
+            lambda d, c=c: wn.at[d, pl.ds(END * c, END)],
+        )
+        for c, s in enumerate((2, 7, 10, 11)[:PIECES])
+    ]
+    h_start, h_arrive, h_sent = exchange(1, lambda d: hb, lambda d: hn.at[d])
+    u_start, u_arrive, u_sent = exchange(3, lambda d: uvb.at[0], lambda d: uvn.at[d])
+    v_start, v_arrive, v_sent = exchange(5, lambda d: uvb.at[1], lambda d: uvn.at[5 + d])
+    b_start, b_arrive, b_sent = exchange(
+        4, lambda d: bsb.at[half[d]], lambda d: bsp.at[yours] if d == 4 else bsn.at[d]
+    )
+
+    def face_send(k, src, dst):
+        copy = remote(src, dst, fsend.at[k], frecv.at[k], other)
+        copy.start()
+        Once(copy.wait_send, finish)
+        return Once(copy.wait_recv, finish)
+
+    for c, (start, _, _) in enumerate(q_sends):
+        get_r0[c].wait()
+        q0[pieces[c], :] = r0[pieces[c], :].astype(BF16)
+        if c == 0:
+            pl.semaphore_wait(barrier, len(x_peers) + len(y_peers))
+        start()
     for d, there in enumerate(gets[:4]):
         @pl.when(jnp.logical_not(there))
         def _():
@@ -141,70 +207,6 @@
             mup[d] = jnp.zeros_like(mup[d])
             hup[d] = jnp.zeros_like(hup[d])
 
-    def exchange(stage, src_of, dst_of):
-        receipts, departures = {}, {}
-
-        def copy(d):
-            k = stage * 5 + d
-            return remote(src_of(d), dst_of(d), esend.at[k], erecv.at[k], target[d])
-
-        def start(order=(4, 0, 1, 2, 3)):
-            for d in order:
-                guarded(sends[d], lambda: copy(d).start())
-                receipts[d] = Once(lambda d=d: guarded(gets[d], copy(d).wait_recv), finish)
-                departures[d] = Once(lambda d=d: guarded(sends[d], copy(d).wait_send), finish)
-
-        def arrive(order=(0, 1, 2, 3)):
-            for d in order:
-                receipts[d].wait()
-
-        def sent(order):
-            for d in order:
-                departures[d].wait()
-
-        return start, arrive, sent
-
-    low, high = pl.ds(0, HALF), pl.ds(HALF, HALF)
-    mine = pl.ds(pl.multiple_of(f * HALF, HALF), HALF)
-    yours = pl.ds(pl.multiple_of((1 - f) * HALF, HALF), HALF)
-    half = (low, high, low, high, yours)
-    chunks = [pl.ds(HALF * c, HALF) for c in range(2)]
-    q_sends = [
-        exchange(s, lambda d, c=c: q0.at[chunks[c]], lambda d, c=c: qn.at[d, chunks[c]])
-        for c, s in enumerate((0, 6))
-    ]
-
-    def ends_of(d, c):
-        shift = (0, QUARTER, 0, QUARTER, (1 - f) * QUARTER)[d]
-        return pl.ds(pl.multiple_of(HALF * c + shift, QUARTER), QUARTER)
-
-    w_sends = [
-        exchange(
-            s,
-            lambda d, c=c: wb.at[ends_of(d, c)],
-            lambda d, c=c: wn.at[d, pl.ds(QUARTER * c, QUARTER)],
-        )
-        for c, s in enumerate((2, 7))
-    ]
-    h_start, h_arrive, h_sent = exchange(1, lambda d: hb, lambda d: hn.at[d])
-    u_start, u_arrive, u_sent = exchange(3, lambda d: uvb.at[0], lambda d: uvn.at[d])
-    v_start, v_arrive, v_sent = exchange(5, lambda d: uvb.at[1], lambda d: uvn.at[5 + d])
-    b_start, b_arrive, b_sent = exchange(
-        4, lambda d: bsb.at[half[d]], lambda d: bsp.at[yours] if d == 4 else bsn.at[d]
-    )
-
-    def face_send(k, src, dst):
-        copy = remote(src, dst, fsend.at[k], frecv.at[k], other)
-        copy.start()
-        Once(copy.wait_send, finish)
-        return Once(copy.wait_recv, finish)
-
-    for c, (start, _, _) in enumerate(q_sends):
-        get_r0[c].wait()
-        q0[chunks[c], :] = r0[chunks[c], :].astype(BF16)
-        if c == 0:
-            pl.semaphore_wait(barrier, len(x_peers) + len(y_peers))
-        start()
     small = [
         load(md.at[0, 0], mw.at[0]), load(mx.at[0, 0], mw.at[1]), load(my.at[0, 0], mw.at[2]),
         load(mp.at[0], mw.at[3]),
@@ -258,14 +260,14 @@
         total = total - wx * nb[0, rows, cols].astype(F32) - ux * nb[1, rows, cols].astype(F32)
         return total - wy * nb[2, rows, cols].astype(F32) - uy * nb[3, rows, cols].astype(F32)
 
-    for c in range(2):
+    for c in range(PIECES):
         start, arrive, sent = q_sends[c]
         arrive()
 
         def body(rows):
             w0[rows, :] = near(w0[rows, :], mw, mup, q0[rows, :].astype(F32), qn, rows)
 
-        row_loop(body, HALF, HALF * c)
+        row_loop(body, PIECE, PIECE * c)
         arrive((4,))
 
         def body(rows):
@@ -273,11 +275,9 @@
             w0[rows, :] = w
             wb[rows, :] = w.astype(BF16)
 
-        row_loop(body, HALF, HALF * c)
+        row_loop(body, PIECE, PIECE * c)
         if c == 0:
-            q_sends[1][2]((4,))
-        else:
-            w_sends[0][2]((4,))
+            q_sends[-1][2]((4,))
         w_sends[c][0]()
     u_start((0, 1))
     h_start((0, 1))
@@ -346,21 +346,23 @@
 
     xm[...] = times(wb[...], zf[...])
     moments(0, r0, w0, wb, xm, mw)
-    w_sends[1][2]((4,))
-    h_start((4, 2, 3))
+    w_sends[-1][2]((4,))
     u_start((4, 2, 3))
-    for c in range(2):
+    v_start((4, 2, 3))
+    for c in range(PIECES):
         w_sends[c][1]()
-        edges(wb, wn, mw, mup, HALF * c, QUARTER * c, QUARTER)
+        edges(wb, wn, mw, mup, PIECE * c, END * c, END)
         w_sends[c][1]((4,))
-        face_edges(wb, lambda rows, own: wn[4, rows, :], mw, HALF * c, QUARTER * c, QUARTER)
+        face_edges(wb, lambda rows, own: wn[4, rows, :], mw, PIECE * c, END * c, END)
     moments_end(0)
     sum_arx1 = sum_start(arx1, x_slot, x_peers, 0)
-    v_start((4, 2, 3))
+    h_start((4, 2, 3))
 
     for k in range(2):
         cols = slice(256 * k, 256 * k + 256)
         buv[:, cols] = times_t(times(uvb[k], bf[...]).astype(BF16), bf[...])
+    mom[1] = sum_arx1()
+    sum_ary1 = sum_start(ary1, y_slot, y_peers, 1)
     h_arrive((0, 1, 2, 3, 4))
 
     def body(rows):
@@ -368,8 +370,6 @@
         bh[rows, :] = total - hw[3] * hn[4, rows, :].astype(F32)
 
     row_loop(body)
-    mom[1] = sum_arx1()
-    sum_ary1 = sum_start(ary1, y_slot, y_peers, 1)
     u_arrive((0, 1, 2, 3, 4))
     v_arrive((0, 1, 2, 3, 4))
 
@@ -516,7 +516,7 @@
                 vm(128, 128), vm(128, 128), vm(5, 128, 128), vm(4, 8, 128),
                 vm(nx, 8, 128), vm(ny * 2, 8, 128), vm(nx, 8, 128), vm(ny * 2, 8, 128),
                 vm(128, 768), vm(128, 256), vm(2, 8, 128), vm(8, 128),
-                sems((64,)), sems((4,)), sems((4,)), sems((40,)), sems((40,)),
+                sems((128,)), sems((4,)), sems((4,)), sems((60,)), sems((60,)),
                 sems((4,)), sems((4,)), sems((3,)), sems((3,)),
             ],
             compiler_params=pltpu.CompilerParams(

time: 70.8 us -> 70.6 us (level)
  no operation moved by 1% of the time
where the time goes in v4:
time: 70.6 us; the launch traced here: 70.4 us
  Pallas kernels  69.7 us (99%)
    pallas_call x1, Pallas kernels, on_device(): pl.pallas_call(functools.partial(kernel, nx, ny, xs, zs), out_shape=outs,...  68.9 us

profile of v4, /device:TPU:1, one launch (start us, length us, event | category | flops | bytes accessed | tf_op | source)
XLA Modules:
  0.0 70.4 jit_solution(10817558382068906296)
XLA Ops:
  0.6 68.9 %shard_map.193 = (f32[1,1,1,128,768]{4,3,2,1,0:T(8,128)S(1)}, f32[1,1,1,128,256]{4,3,2,1,0:T(8,128)S(1)}, f32[1,1,128]{2,1,0:T(1,128)S(1)}) custom-call(f32[1,1,1,128,768]{4,3,2,1,0:T(8,128)} %ml.1, f32[1,1,1,128,256]{4,3,2,1,0:T(8,128)} %hl.1, bf16[1,1,1,768,768]{4,3,2,1,0:T(8,128)(2,1)} %mf.1, bf16[1,1,1,256,256]{4,3,2,1,0:T(8,128)(2,1)} %hf.1, ...), custom_call_target="tpu_custom_call" | custom-call | tf_op jit(solution)/shard_map/pallas_call | solution.py:501
  69.6 0.8 %shard_map.194 = (f32[1,1,1,128,768]{4,3,2,1,0:T(8,128)}, f32[1,1,1,128,256]{4,3,2,1,0:T(8,128)}, f32[1,1,128]{2,1,0:T(1,128)}) custom-call(f32[1,1,1,128,768]{4,3,2,1,0:T(8,128)S(1)} %get-tuple-element.6.a, f32[1,1,1,128,256]{4,3,2,1,0:T(8,128)S(1)} %get-tuple-element.7.b, f32[1,1,128]{2,1,0:T(1,128)S(1)} %get-tuple-element.8.c), custom_call_target="tpu_custom_call" | custom-call | tf_op jit(solution)/shard_map/pallas_call | solution.py:526
